TPU v7x, 32 devices: a whole 2x2x4 slice. The times are simulated.
32 devices in a mesh: sec: 8 (over z, y), tile: 4 (over x, core).
Axes of the slice: x: 2, y: 2, z: 4, core: 2. Of those that a mesh axis runs over, the one named last changes fastest.
Arguments:
- images: bfloat16 [16, 128, 256], P('sec', 'tile'), may hold values from -6 to 6
- seam_links: int32 [16, 3], replicated, may hold values 0 or 1
- partners: int32 [16, 3], P('sec'), may hold values from 0 to 15, as said below
- enc_first: bfloat16 [64, 1, 3, 3], replicated, may hold values from -3 to 3
- enc_second: bfloat16 [64, 64, 3, 3], replicated, may hold values from -0.375 to 0.375
- enc_third: bfloat16 [32, 64, 1, 1], replicated, may hold values from -1 to 1
- dec_first: bfloat16 [64, 81, 3, 3], replicated, may hold values from -0.3125 to 0.3125
- dec_second: bfloat16 [64, 64, 3, 3], replicated, may hold values from -0.375 to 0.375
- dec_third: bfloat16 [2, 64, 3, 3], replicated, may hold values from -0.375 to 0.375
Outputs:
- descriptors: bfloat16 [16, 32, 64, 128], P('sec', None, 'tile')
- flows: float32 [16, 3, 2, 64, 128], P('sec', None, None, 'tile')
Inputs may be any that keep to these rules, and one draw needn't show every extreme that they name: partners[s, j] is s + o or s - o, with o = 1, 2, 4 for j = 0, 1, 2.
All inputs are finite; a program needn't handle non-finite values.
Results may differ from a plain program's by a relative error of at most 0.0098.
Values may be sent and summed in bfloat16 or wider, within the bound.
No kernel may reach another device: no remote copies, remote signals or barrier semaphores. Data moves between devices by JAX's collectives and lax.ppermute only.
A program may use at most 128 MiB of HBM per device.

v0:
```python
import functools
import math

import jax
import jax.numpy as jnp
from jax import lax
from jax.experimental import pallas as pl
from jax.experimental.pallas import tpu as pltpu
from jax.sharding import PartitionSpec as P

RADIUS = 4
WINDOW = 2 * RADIUS + 1
SLOPE = 0.1
OFFSETS = (1, 2, 4)

f32 = jnp.float32
bf16 = jnp.bfloat16


def dot(a, b):
    return jnp.dot(a, b, preferred_element_type=f32)


def leaky(v):
    return jnp.maximum(v, SLOPE * v)


def iota(shape, dim):
    return lax.broadcasted_iota(jnp.int32, shape, dim)


def col_shift(v, by):
    width = v.shape[-1]
    rolled = pltpu.roll(v, (-by) % width, axis=v.ndim - 1)
    x = iota(v.shape, v.ndim - 1) + by
    return jnp.where((x >= 0) & (x < width), rolled, 0.0)


def stack_cols(v, by):
    return jnp.concatenate(
        [col_shift(v, -by).astype(bf16), v.astype(bf16), col_shift(v, by).astype(bf16)], axis=0
    )


def onehot(shape, cond):
    return jnp.where(cond, 1.0, 0.0).astype(bf16)


def body(
    meta_ref, links_ref, partners_ref, img_ref, ha_ref, hb_ref,
    w1_ref, w2_ref, w3_ref, d1_ref, d2_ref, d3_ref,
    desc_ref, flow_ref,
    ext, sel, w1t, w2c, d1c, d2c, d3c, dmap, own, cost,
):
    here = img_ref.shape[0] // 6
    n_seam = links_ref.shape[1]
    sec = meta_ref[0]
    tile = meta_ref[1]
    desc_ch = w3_ref.shape[0]
    enc_ch = w3_ref.shape[1]
    width = desc_ref.shape[3]
    in_width = img_ref.shape[2]

    r = iota((in_width, 3 * width), 0)
    q = iota((in_width, 3 * width), 1)
    sel[...] = onehot(None, r == 2 * (q % width) + q // width - 1)
    j = iota((9, 8 * 128), 0)
    lane = iota((9, 8 * 128), 1)
    m, kx, ql = lane // 128, (lane % 128) // 32, lane % 32
    place = onehot(None, (j % 3 == kx) & (ql == 2 * m + j // 3))
    spread = lax.dot_general(
        w1_ref[...], place, (((0,), (0,)), ((), ())), preferred_element_type=f32
    ).astype(bf16)
    for i in range(8):
        w1t[enc_ch * i : enc_ch * (i + 1), :] = spread[:, 128 * i : 128 * (i + 1)]
    disp = d1_ref.shape[2]
    main = disp - 1
    r = iota((disp, 256), 0)
    q = iota((disp, 256), 1)
    for ky in range(3):
        acc = jnp.zeros((enc_ch, 256), f32)
        for kx in range(3):
            put = onehot(None, ((r < main) & (q == kx * main + r)) | ((r == main) & (q == 3 * main + kx)))
            acc = acc + dot(d1_ref[3 * ky + kx], put)
        d1c[enc_ch * ky : enc_ch * (ky + 1), :] = acc.astype(bf16)
        r2 = iota((enc_ch, 3 * enc_ch), 0)
        q2 = iota((enc_ch, 3 * enc_ch), 1)
        for src, dst, pitch in ((w2_ref, w2c, enc_ch), (d2_ref, d2c, enc_ch), (d3_ref, d3c, 8)):
            rows = src.shape[1]
            acc = jnp.zeros((rows, 3 * enc_ch), f32)
            for kx in range(3):
                acc = acc + dot(src[3 * ky + kx], onehot(None, q2 == kx * enc_ch + r2))
            dst[pitch * ky : pitch * ky + rows, :] = acc.astype(dst.dtype)
    cost[...] = jnp.zeros_like(cost)

    def link(section, seam):
        inside = (seam >= 0) & (seam < n_seam)
        value = links_ref[section, jnp.clip(seam, 0, n_seam - 1)]
        return jnp.where(inside, value, 0).astype(f32)

    def encode(cand, low, up):
        height = img_ref.shape[1]

        @pl.when(tile % 2 == 0)
        def _():
            ext[0:height, :] = hb_ref[cand]
            ext[2 * height : 3 * height, :] = ha_ref[cand]

        @pl.when(tile % 2 == 1)
        def _():
            ext[0:height, :] = ha_ref[cand]
            ext[2 * height : 3 * height, :] = hb_ref[cand]

        ext[height : 2 * height, :] = img_ref[cand]
        taps = dot(ext[...], sel[...]).astype(bf16)
        down = onehot(None, iota((112, 96), 0) == iota((112, 96), 1) + 1)
        taps = dot(down, taps).astype(bf16)
        blank = jnp.zeros((32, width), bf16)

        def window(first, factor=None):
            parts = []
            for kx in range(3):
                part = taps[first : first + 32, kx * width : (kx + 1) * width]
                if factor is not None:
                    scale = jnp.where(iota((32, width), 0) == 0, factor, 1.0)
                    part = (part.astype(f32) * scale).astype(bf16)
                parts.append(part)
            return jnp.concatenate(parts + [blank], axis=0)

        feats = {}

        def keep(out, first, lane0):
            for i in range(out.shape[0] // enc_ch):
                v = leaky(out[enc_ch * i : enc_ch * (i + 1), lane0 : lane0 + width])
                feats[first + i] = stack_cols(v, 2)

        keep(dot(w1t[6 * enc_ch :, :], window(0)), -10, 0)
        pair = dot(w1t[...], jnp.concatenate([window(16), window(32, low)], axis=1))
        keep(pair, -8, 0)
        keep(pair, 0, width)
        pair = dot(w1t[...], jnp.concatenate([window(48), window(64, up)], axis=1))
        keep(pair, 8, 0)
        keep(pair, 16, width)
        keep(dot(w1t[: 2 * enc_ch, :], window(80)), 24, 0)

        parts = {}
        for p in range(-5, 13):
            x = jnp.concatenate([feats[2 * p], feats[2 * p + 1]], axis=1)
            if p == -5:
                parts[p] = (dot(w2c[:enc_ch, :], x), None, None)
            elif p == 12:
                parts[p] = (None, None, dot(w2c[2 * enc_ch :, :], x))
            else:
                t = dot(w2c[...], x)
                parts[p] = (t[:enc_ch], t[enc_ch : 2 * enc_ch], t[2 * enc_ch :])
            o = p - 1
            if o < -4:
                continue
            before, mid, after = parts[o - 1][0], parts[o][1], parts[o + 1][2]
            if o == 0:
                before = before * low
            if o == 8:
                before = before * up
            if o == -1:
                after = after * low
            if o == 7:
                after = after * up
            second = leaky(before + mid + after).astype(bf16)
            d = dot(w3_ref[...], second).astype(bf16).astype(f32)
            for half in range(2):
                row = 2 * o + half + 8
                dmap[pl.ds(row, desc_ch, stride=32), :] = d[:, half * width : (half + 1) * width]

    def correlate(low_p, up_p, low_s, up_s):
        for k in range(3):
            y = iota((8, width), 0) + (8 * k - RADIUS)
            self_mask = jnp.where(y < 0, low_s, jnp.where(y >= 16, up_s, 1.0)) * (
                1.0 / math.sqrt(desc_ch)
            )
            for g in range(3):
                init = tuple(jnp.zeros((8, width), f32) for _ in range(27))

                def step(c, acc, k=k, g=g):
                    acc = list(acc)
                    mine = [
                        own[3 * g + b, pl.ds(pl.multiple_of(c * 24, 8) + 8 * k, 8), :]
                        for b in range(3)
                    ]
                    for a in range(9):
                        other = dmap[pl.ds(c * 32 + 8 * k + a, 8), :]
                        for b in range(3):
                            acc[3 * a + b] = acc[3 * a + b] + mine[b] * other
                    return tuple(acc)

                acc = lax.fori_loop(0, desc_ch, step, init, unroll=4)
                for a in range(9):
                    yp = y + (a - RADIUS)
                    mask = self_mask
                    if k == 0:
                        mask = jnp.where((y < 0) != (yp < 0), mask * low_p, mask)
                    if k == 2:
                        mask = jnp.where((y < 16) != (yp < 16), mask * up_p, mask)
                    for b in range(3):
                        by = 3 * g + b - RADIUS
                        v = col_shift(acc[3 * a + b] * mask, by)
                        d = a * WINDOW + 3 * g + b
                        if d < WINDOW * WINDOW - 1:
                            cost[pl.ds(8 * k * 96 + d, 8, stride=96), :] = v
                        else:
                            for i, s in enumerate((-1, 0, 1)):
                                moved = v if s == 0 else col_shift(v, s)
                                cost[pl.ds(8 * k * 96 + d + i, 8, stride=96), :] = moved

    def decode(sec_i, slot, low_s, up_s):
        def rows_of(t, pitch, base):
            pass

        t1 = {}
        for p in range(-2, 10):
            halves = []
            for row in (2 * p, 2 * p + 1):
                at = (row + RADIUS) * 96
                v = cost[at : at + 96, :]
                v80 = v[:80].astype(bf16).astype(f32)
                halves.append(
                    jnp.concatenate([stack_cols(v80, 1), v[80:96].astype(bf16)], axis=0)
                )
            t = dot(d1c[...], jnp.concatenate(halves, axis=1))
            t1[2 * p] = t[:, :width]
            t1[2 * p + 1] = t[:, width:]

        def join(t, row, pitch, n):
            return (
                t[row - 1][:n] + t[row][pitch : pitch + n] + t[row + 1][2 * pitch : 2 * pitch + n]
            )

        def hidden(t, row):
            v = leaky(join(t, row, enc_ch, enc_ch))
            if row < 0:
                v = v * low_s
            if row >= 16:
                v = v * up_s
            return stack_cols(v, 1)

        t2 = {}
        for p in range(-1, 9):
            x = jnp.concatenate([hidden(t1, 2 * p), hidden(t1, 2 * p + 1)], axis=1)
            t = dot(d2c[...], x)
            t2[2 * p] = t[:, :width]
            t2[2 * p + 1] = t[:, width:]
        t3 = {}
        for p in range(9):
            x = jnp.concatenate([hidden(t2, 2 * p - 1), hidden(t2, 2 * p)], axis=1)
            t = dot(d3c[...].astype(bf16), x)
            t3[2 * p - 1] = t[:, :width]
            t3[2 * p] = t[:, width:]
        for row in range(16):
            v = join(t3, row, 8, 2)
            for o in range(2):
                flow_ref[sec_i, slot, o, row : row + 1, :] = v[o : o + 1, :]

    def section(sec_i, carry):
        mine = sec * here + sec_i
        low_s = link(mine, tile - 1)
        up_s = link(mine, tile)
        encode(sec_i, low_s, up_s)

        def keep_own(c, carry):
            v = dmap[pl.ds(c * 32 + RADIUS, 24), :]
            at = pl.multiple_of(c * 24, 8)
            for b in range(WINDOW):
                by = (b - RADIUS) % width
                own[b, pl.ds(at, 24), :] = pltpu.roll(v, by, axis=1) if by else v
            desc_ref[sec_i, c] = v[RADIUS : RADIUS + 16].astype(bf16)
            return carry

        lax.fori_loop(0, desc_ch, keep_own, 0)

        def pair(slot, carry):
            other = partners_ref[sec_i, slot]
            dev = other // here
            away = (dev // 2) - (sec // 2)
            near_a = (dev // 2) == ((sec // 2) ^ 1)
            block = jnp.where(away == 0, 0, jnp.where(near_a, 1, 2))
            twin = jnp.where(dev % 2 == sec % 2, 0, 1)
            cand = (block * 2 + twin) * here + other % here
            low_p = link(other, tile - 1)
            up_p = link(other, tile)
            encode(cand, low_p, up_p)
            correlate(low_p, up_p, low_s, up_s)
            decode(sec_i, slot, low_s, up_s)
            return carry

        return lax.fori_loop(0, len(OFFSETS), pair, carry)

    lax.fori_loop(0, here, section, 0)


def swap(x, axis, first, stride=1):
    size = lax.axis_size(axis)
    route = []
    for i in range(first * stride, size - stride):
        if (i // stride - first) % 2 == 0:
            route += [(i, i + stride), (i + stride, i)]
    return lax.ppermute(x, axis, route)


def shards(
    images, seam_links, partners, enc_first, enc_second, enc_third, dec_first, dec_second, dec_third
):
    here, height, in_width = images.shape
    assert here * 2 >= max(OFFSETS) and lax.axis_size("sec") % 2 == 0
    meta = jnp.stack([lax.axis_index("sec"), lax.axis_index("tile")]).astype(jnp.int32)
    near = jnp.concatenate([images, swap(images, "sec", 0)], axis=0)
    cands = jnp.concatenate([near, swap(near, "sec", 0, 2), swap(near, "sec", 1, 2)], axis=0)
    ha = swap(cands, "tile", 0)
    hb = swap(cands, "tile", 1)

    def taps(w):
        return jnp.transpose(w, (2, 3, 0, 1)).reshape((-1,) + w.shape[:2])

    w1 = jnp.transpose(enc_first, (1, 2, 3, 0)).reshape(9, -1)
    w3 = enc_third[:, :, 0, 0]
    enc_ch = enc_first.shape[0]
    desc_ch = enc_third.shape[0]
    rows, width = height // 2, in_width // 2
    smem = pl.BlockSpec(memory_space=pltpu.SMEM)
    vmem = pl.BlockSpec(memory_space=pltpu.VMEM)
    return pl.pallas_call(
        body,
        in_specs=[smem] * 3 + [vmem] * 9,
        out_specs=[vmem] * 2,
        out_shape=[
            jax.ShapeDtypeStruct((here, desc_ch, rows, width), bf16),
            jax.ShapeDtypeStruct((here, len(OFFSETS), dec_third.shape[0], rows, width), f32),
        ],
        scratch_shapes=[
            pltpu.VMEM((3 * height, in_width), bf16),
            pltpu.VMEM((in_width, 3 * width), bf16),
            pltpu.VMEM((8 * enc_ch, 128), bf16),
            pltpu.VMEM((3 * enc_ch, 3 * enc_ch), bf16),
            pltpu.VMEM((3 * enc_ch, 256), bf16),
            pltpu.VMEM((3 * enc_ch, 3 * enc_ch), bf16),
            pltpu.VMEM((24, 3 * enc_ch), f32),
            pltpu.VMEM((desc_ch * 32, width), f32),
            pltpu.VMEM((WINDOW, desc_ch * 24, width), f32),
            pltpu.VMEM((24 * 96, width), f32),
        ],
        compiler_params=pltpu.CompilerParams(vmem_limit_bytes=48 * 1024 * 1024),
    )(meta, seam_links, partners, cands, ha, hb, w1, taps(enc_second), w3, taps(dec_first),
      taps(dec_second), taps(dec_third))


def solution(mesh):
    return jax.shard_map(
        shards,
        mesh=mesh,
        in_specs=(P("sec", "tile", None), P(), P("sec", None), P(), P(), P(), P(), P(), P()),
        out_specs=(P("sec", None, "tile", None), P("sec", None, None, "tile", None)),
        check_vma=False,
    )
```

profile of v0, /device:TPU:17, one launch (start us, length us, event | category | flops | bytes accessed | tf_op | source)
XLA Modules:
  0.0 79.4 jit_solution(5417744430084783742)
XLA Ops:
  0.6 1.3 %collective-permute-start = (bf16[2,32,256]{2,1,0:T(8,128)(2,1)}, bf16[2,32,256]{2,1,0:T(8,128)(2,1)S(1)}, u32[]{:S(2)}, u32[]{:S(2)}) collective-permute-start(bf16[2,32,256]{2,1,0:T(8,128)(2,1)} %param.9), channel_id=1, source_target_pairs={{0,4},{4,0},{8,12},{12,8},{16,20},{20,16},{24,28},{28,24},{1,5},{5... | collective-permute-start | bytes 98312 | tf_op jit(solution)/shard_map/ppermute | solution.py:305
  1.9 0.8 %constant_dynamic-update-slice_fusion.1 = (bf16[4,32,256]{2,1,0:T(8,128)(2,1)S(1)}, bf16[12,32,256]{2,1,0:T(8,128)(2,1)S(1)}) fusion(bf16[2,32,256]{2,1,0:T(8,128)(2,1)} %param.9), kind=kLoop, calls=%fused_computation.1 | loop fusion | bytes 98304
  2.8 0.9 %collective-permute-done = bf16[2,32,256]{2,1,0:T(8,128)(2,1)S(1)} collective-permute-done((bf16[2,32,256]{2,1,0:T(8,128)(2,1)}, bf16[2,32,256]{2,1,0:T(8,128)(2,1)S(1)}, u32[]{:S(2)}, u32[]{:S(2)}) %collective-permute-start) | collective-permute-done | bytes 32800 | tf_op jit(solution)/shard_map/ppermute | solution.py:305
  3.7 1.4 %collective-permute-start.1 = (bf16[4,32,256]{2,1,0:T(8,128)(2,1)S(1)}, bf16[4,32,256]{2,1,0:T(8,128)(2,1)S(1)}, u32[]{:S(2)}, u32[]{:S(2)}) collective-permute-start(bf16[4,32,256]{2,1,0:T(8,128)(2,1)S(1)} %get-tuple-element.2), channel_id=1, source_target_pairs={{0,8},{8,0},{4,12},{12,4},{16,24},{24,16},{20,28},{28,20},{1,9},{9... | collective-permute-start | bytes 196616 | tf_op jit(solution)/shard_map/ppermute | solution.py:305
  5.0 1.9 %collective-permute-start.2 = (bf16[4,32,256]{2,1,0:T(8,128)(2,1)S(1)}, bf16[4,32,256]{2,1,0:T(8,128)(2,1)S(1)}, u32[]{:S(2)}, u32[]{:S(2)}) collective-permute-start(bf16[4,32,256]{2,1,0:T(8,128)(2,1)S(1)} %get-tuple-element.2), channel_id=1, source_target_pairs={{8,16},{16,8},{12,20},{20,12},{9,17},{17,9},{13,21},{21,13},{10,18... | collective-permute-start | bytes 196616 | tf_op jit(solution)/shard_map/ppermute | solution.py:305
  7.0 0.0 collective-permute-done.1
  7.0 0.0 copy-start
  7.0 0.0 copy-start.1
  7.0 3.0 %collective-permute-done.2 = bf16[4,32,256]{2,1,0:T(8,128)(2,1)S(1)} collective-permute-done((bf16[4,32,256]{2,1,0:T(8,128)(2,1)S(1)}, bf16[4,32,256]{2,1,0:T(8,128)(2,1)S(1)}, u32[]{:S(2)}, u32[]{:S(2)}) %collective-permute-start.2) | collective-permute-done | bytes 65568 | tf_op jit(solution)/shard_map/ppermute | solution.py:305
  10.1 6.2 %collective-permute-start.4 = (bf16[12,32,256]{2,1,0:T(8,128)(2,1)S(1)}, bf16[12,32,256]{2,1,0:T(8,128)(2,1)S(1)}, u32[]{:S(2)}, u32[]{:S(2)}) collective-permute-start(bf16[12,32,256]{2,1,0:T(8,128)(2,1)S(1)} %constant_dynamic-update-slice_fusion.2.img_ref), channel_id=1, source_target_pairs={{1,2},{2,1},{5,6},{6,5},{9,10},{10,9},{13,14},{14,13},{17,18},{18,... | collective-permute-start | bytes 589832 | tf_op jit(solution)/shard_map/ppermute | solution.py:305
  16.3 0.1 collective-permute-start.3
  16.4 0.0 copy-done.6
  16.4 0.0 copy-done.7
  16.4 0.1 copy.11.links_ref
  16.5 0.1 pad_add_fusion.meta_ref
  16.6 3.1 %collective-permute-done.4.hb_ref = bf16[12,32,256]{2,1,0:T(8,128)(2,1)S(1)} collective-permute-done((bf16[12,32,256]{2,1,0:T(8,128)(2,1)S(1)}, bf16[12,32,256]{2,1,0:T(8,128)(2,1)S(1)}, u32[]{:S(2)}, u32[]{:S(2)}) %collective-permute-start.4) | collective-permute-done | bytes 196640 | tf_op jit(solution)/shard_map/ppermute | solution.py:305
  19.6 0.0 collective-permute-done.3.ha_ref
  19.6 0.0 copy-done.2
  19.7 0.0 copy-done.5
  19.7 0.0 copy-done
  19.7 0.0 copy-done.1
  19.7 0.0 copy-done.3
  19.7 0.0 copy-done.4
  19.7 59.7 %shard_map.104 = (bf16[2,32,16,128]{3,2,1,0:T(8,128)(2,1)}, f32[2,3,2,16,128]{4,3,2,1,0:T(8,128)}) custom-call(s32[2]{0:T(128)S(1)} %pad_add_fusion.meta_ref, s32[16,3]{1,0:T(8,128)S(1)} %copy.11.links_ref, s32[2,3]{1,0:T(2,128)S(1)} %copy-done.5, bf16[12,32,256]{2,1,0:T(8,128)(2,1)S(1)} %constant_dynamic-update-slice_fusion.2.img_ref, ...), custom_call_target="tpu_custom_call" | custom-call | tf_op jit(solution)/shard_map/pallas_call | solution.py:329
  (10 shorter events, 0.0 us)
Async XLA Ops:
  0.6 3.0 %collective-permute-start = (bf16[2,32,256]{2,1,0:T(8,128)(2,1)}, bf16[2,32,256]{2,1,0:T(8,128)(2,1)S(1)}, u32[]{:S(2)}, u32[]{:S(2)}) collective-permute-start(bf16[2,32,256]{2,1,0:T(8,128)(2,1)} %param.9), channel_id=1, source_target_pairs={{0,4},{4,0},{8,12},{12,8},{16,20},{20,16},{24,28},{28,24},{1,5},{5... | collective-permute-start | bytes 98312 | tf_op jit(solution)/shard_map/ppermute | solution.py:305
  1.9 17.7 %copy-start.2 = (bf16[64,64,3,3]{1,0,3,2:T(8,128)(2,1)S(1)}, bf16[64,64,3,3]{1,0,3,2:T(8,128)(2,1)}, u32[]{:S(2)}) copy-start(bf16[64,64,3,3]{1,0,3,2:T(8,128)(2,1)} %param.16) | copy-start | bytes 221188
  3.7 12.7 %copy-start.6 = (bf16[64,1,3,3]{0,3,2,1:T(4,128)(2,1)S(1)}, bf16[64,1,3,3]{0,3,2,1:T(4,128)(2,1)}, u32[]{:S(2)}) copy-start(bf16[64,1,3,3]{0,3,2,1:T(4,128)(2,1)} %param.12) | copy-start | bytes 3460
  3.7 12.7 %copy-start.7 = (s32[16,3]{0,1:T(4,128)S(1)}, s32[16,3]{0,1:T(4,128)}, u32[]{:S(2)}) copy-start(s32[16,3]{0,1:T(4,128)} %param.10) | copy-start | bytes 580
  3.7 16.0 %copy-start.5 = (s32[2,3]{1,0:T(2,128)S(1)}, s32[2,3]{1,0:T(2,128)}, u32[]{:S(2)}) copy-start(s32[2,3]{1,0:T(2,128)} %partners_ref.1) | copy-start | bytes 76
  3.7 3.3 %collective-permute-start.1 = (bf16[4,32,256]{2,1,0:T(8,128)(2,1)S(1)}, bf16[4,32,256]{2,1,0:T(8,128)(2,1)S(1)}, u32[]{:S(2)}, u32[]{:S(2)}) collective-permute-start(bf16[4,32,256]{2,1,0:T(8,128)(2,1)S(1)} %get-tuple-element.2), channel_id=1, source_target_pairs={{0,8},{8,0},{4,12},{12,4},{16,24},{24,16},{20,28},{28,20},{1,9},{9... | collective-permute-start | bytes 196616 | tf_op jit(solution)/shard_map/ppermute | solution.py:305
  5.0 5.0 %collective-permute-start.2 = (bf16[4,32,256]{2,1,0:T(8,128)(2,1)S(1)}, bf16[4,32,256]{2,1,0:T(8,128)(2,1)S(1)}, u32[]{:S(2)}, u32[]{:S(2)}) collective-permute-start(bf16[4,32,256]{2,1,0:T(8,128)(2,1)S(1)} %get-tuple-element.2), channel_id=1, source_target_pairs={{8,16},{16,8},{12,20},{20,12},{9,17},{17,9},{13,21},{21,13},{10,18... | collective-permute-start | bytes 196616 | tf_op jit(solution)/shard_map/ppermute | solution.py:305
  7.0 12.7 %copy-start = (bf16[64,64,3,3]{1,0,3,2:T(8,128)(2,1)S(1)}, bf16[64,64,3,3]{1,0,3,2:T(8,128)(2,1)}, u32[]{:S(2)}) copy-start(bf16[64,64,3,3]{1,0,3,2:T(8,128)(2,1)} %param.13) | copy-start | bytes 221188
  7.0 12.7 %copy-start.1 = (bf16[64,81,3,3]{1,0,3,2:T(8,128)(2,1)S(1)}, bf16[64,81,3,3]{1,0,3,2:T(8,128)(2,1)}, u32[]{:S(2)}) copy-start(bf16[64,81,3,3]{1,0,3,2:T(8,128)(2,1)} %param.15) | copy-start | bytes 279940
  10.1 9.6 %collective-permute-start.4 = (bf16[12,32,256]{2,1,0:T(8,128)(2,1)S(1)}, bf16[12,32,256]{2,1,0:T(8,128)(2,1)S(1)}, u32[]{:S(2)}, u32[]{:S(2)}) collective-permute-start(bf16[12,32,256]{2,1,0:T(8,128)(2,1)S(1)} %constant_dynamic-update-slice_fusion.2.img_ref), channel_id=1, source_target_pairs={{1,2},{2,1},{5,6},{6,5},{9,10},{10,9},{13,14},{14,13},{17,18},{18,... | collective-permute-start | bytes 589832 | tf_op jit(solution)/shard_map/ppermute | solution.py:305
  16.3 3.3 %collective-permute-start.3 = (bf16[12,32,256]{2,1,0:T(8,128)(2,1)S(1)}, bf16[12,32,256]{2,1,0:T(8,128)(2,1)S(1)}, u32[]{:S(2)}, u32[]{:S(2)}) collective-permute-start(bf16[12,32,256]{2,1,0:T(8,128)(2,1)S(1)} %constant_dynamic-update-slice_fusion.2.img_ref), channel_id=1, source_target_pairs={{0,1},{1,0},{2,3},{3,2},{4,5},{5,4},{6,7},{7,6},{8,9},{9,8},{10,11... | collective-permute-start | bytes 589832 | tf_op jit(solution)/shard_map/ppermute | solution.py:305
  16.5 3.2 %copy-start.3 = (bf16[32,64,1,1]{1,0,3,2:T(8,128)(2,1)S(1)}, bf16[32,64,1,1]{1,0,3,2:T(8,128)(2,1)}, u32[]{:S(2)}) copy-start(bf16[32,64,1,1]{1,0,3,2:T(8,128)(2,1)} %param.14) | copy-start | bytes 12292
  16.6 3.1 %copy-start.4 = (bf16[2,64,3,3]{1,0,3,2:T(2,128)(2,1)S(1)}, bf16[2,64,3,3]{1,0,3,2:T(2,128)(2,1)}, u32[]{:S(2)}) copy-start(bf16[2,64,3,3]{1,0,3,2:T(2,128)(2,1)} %param.17) | copy-start | bytes 6916
where the time goes:
time: 79.6 us; the launch traced here: 79.4 us
  Pallas kernels  59.7 us (75%)
  starting transfers between devices  10.9 us (14%)
  waiting for transfers between devices  7 us (9%)
  local copies, waits for them, and re-layouts  0.98 us (1%)
    pallas_call x1, Pallas kernels, shards(): pl.pallas_call(body, in_specs=[smem] * 3 + [vmem] * 9, out_specs=[vmem] *...  59.7 us
    ppermute x5, starting transfers between devices, swap(): return lax.ppermute(x, axis, route)  10.9 us
    ppermute x5, waiting for transfers between devices, swap(): return lax.ppermute(x, axis, route)  7 us
  transfers between devices with their start and end apart: 5, of which 3 were waited for; matrix products, arithmetic and copies ran while one was open for 1% of the time, Pallas kernels for 0%

commit v1 on v0

v1 whole, which is shorter than its diff:
```python
import functools
import math

import jax
import jax.numpy as jnp
from jax import lax
from jax.experimental import pallas as pl
from jax.experimental.pallas import tpu as pltpu
from jax.sharding import PartitionSpec as P

RADIUS = 4
WINDOW = 2 * RADIUS + 1
SLOPE = 0.1
LAG = 3
OFFSETS = (1, 2, 4)

f32 = jnp.float32
bf16 = jnp.bfloat16


def dot(a, b):
    return jnp.dot(a, b, preferred_element_type=f32)


def leaky(v):
    return jnp.maximum(v, SLOPE * v)


def iota(shape, dim):
    return lax.broadcasted_iota(jnp.int32, shape, dim)


def col_shift(v, by):
    width = v.shape[-1]
    rolled = pltpu.roll(v, (-by) % width, axis=v.ndim - 1)
    x = iota(v.shape, v.ndim - 1) + by
    return jnp.where((x >= 0) & (x < width), rolled, jnp.zeros_like(rolled))


def stack_cols(v, by):
    v = v.astype(bf16)
    return jnp.concatenate([col_shift(v, -by), v, col_shift(v, by)], axis=0)


def onehot(shape, cond):
    return jnp.where(cond, 1.0, 0.0).astype(bf16)


def body(
    meta_ref, links_ref, partners_ref, img_ref, ha_ref, hb_ref,
    w1_ref, w2_ref, w3_ref, d1_ref, d2_ref, d3_ref,
    desc_ref, flow_ref,
    sel, w1t, w2c, d1c, d2c, d3c, dmap_a, dmap_b, own, ownh, win, winh, cost_a, cost_b,
):
    here = img_ref.shape[0] // 6
    n_seam = links_ref.shape[1]
    sec = meta_ref[0]
    tile = meta_ref[1]
    desc_ch = w3_ref.shape[0]
    enc_ch = w3_ref.shape[1]
    width = desc_ref.shape[3]
    in_width = img_ref.shape[2]

    r = iota((in_width, 3 * width), 0)
    q = iota((in_width, 3 * width), 1)
    sel[...] = onehot(None, r == 2 * (q % width) + q // width - 1)
    j = iota((9, 8 * 128), 0)
    lane = iota((9, 8 * 128), 1)
    m, kx, ql = lane // 128, (lane % 128) // 32, lane % 32
    place = onehot(None, (j % 3 == kx) & (ql == 2 * m + j // 3))
    spread = lax.dot_general(
        w1_ref[...], place, (((0,), (0,)), ((), ())), preferred_element_type=f32
    ).astype(bf16)
    for i in range(8):
        w1t[enc_ch * i : enc_ch * (i + 1), :] = spread[:, 128 * i : 128 * (i + 1)]
    disp = d1_ref.shape[2]
    main = disp - 1
    r = iota((disp, 256), 0)
    q = iota((disp, 256), 1)
    for ky in range(3):
        acc = jnp.zeros((enc_ch, 256), f32)
        for kx in range(3):
            put = onehot(None, ((r < main) & (q == kx * main + r)) | ((r == main) & (q == 3 * main + kx)))
            acc = acc + dot(d1_ref[3 * ky + kx], put)
        d1c[enc_ch * ky : enc_ch * (ky + 1), :] = acc.astype(bf16)
        r2 = iota((enc_ch, 3 * enc_ch), 0)
        q2 = iota((enc_ch, 3 * enc_ch), 1)
        for src, dst, pitch in ((w2_ref, w2c, enc_ch), (d2_ref, d2c, enc_ch), (d3_ref, d3c, 8)):
            rows = src.shape[1]
            acc = jnp.zeros((rows, 3 * enc_ch), f32)
            for kx in range(3):
                acc = acc + dot(src[3 * ky + kx], onehot(None, q2 == kx * enc_ch + r2))
            dst[pitch * ky : pitch * ky + rows, :] = acc.astype(dst.dtype)
    for cost in (cost_a, cost_b):
        cost[...] = jnp.zeros_like(cost)
    even = tile % 2 == 0
    one = jnp.where(tile >= 0, 1.0, 0.0).astype(f32)
    pace = {}
    one_row = (jnp.zeros((16, width), f32) + one).astype(bf16)

    def paced(v, by=None):
        tick = pace.get("tick")
        if tick is None:
            return v * (one if by is None else by)
        factor = tick if by is None else tick * by
        return (v.reshape(-1, 8, width) * factor[None]).reshape(v.shape)


    def link(section, seam):
        inside = (seam >= 0) & (seam < n_seam)
        value = links_ref[section, jnp.clip(seam, 0, n_seam - 1)]
        return jnp.where(inside, value, 0).astype(f32)

    def encode(dmap, cand, low, up):
        taps, feats, parts = [], {}, {}
        blank = jnp.zeros((32, width), bf16)

        def start():
            first, second = ha_ref[cand], hb_ref[cand]
            strip = [jnp.where(even, second, first), img_ref[cand], jnp.where(even, first, second)]
            cols = dot(jnp.concatenate(strip, axis=0), sel[...]).astype(bf16)
            down = onehot(None, iota((112, 96), 0) == iota((112, 96), 1) + 1)
            taps.append(dot(down, cols).astype(bf16))

        def window(first, factor=None):
            rows = []
            for kx in range(3):
                part = taps[0][first : first + 32, kx * width : (kx + 1) * width]
                if "tick" in pace and kx == 0:
                    part = paced(part.astype(f32)).astype(bf16)
                if factor is not None:
                    scale = jnp.where(iota((32, width), 0) == 0, factor, 1.0)
                    part = (part.astype(f32) * scale).astype(bf16)
                rows.append(part)
            return jnp.concatenate(rows + [blank], axis=0)

        def conv_first(first_row, lhs, *rhs):
            out = dot(w1t[lhs, :], jnp.concatenate([window(*w) for w in rhs], axis=1))
            for i in range(out.shape[0] // enc_ch):
                for j in range(len(rhs)):
                    feats[first_row + 8 * j + i] = out[
                        enc_ch * i : enc_ch * (i + 1), width * j : width * (j + 1)
                    ]

        def activate(r):
            v = feats[r]
            feats[r] = stack_cols(jnp.maximum(v, paced(v, SLOPE)), 2)

        def conv_second(p):
            x = jnp.concatenate([feats[2 * p], feats[2 * p + 1]], axis=1)
            if p == -5:
                parts[p] = (dot(w2c[:enc_ch, :], x), None, None)
            elif p == 12:
                parts[p] = (None, None, dot(w2c[2 * enc_ch :, :], x))
            else:
                t = dot(w2c[...], x)
                parts[p] = (t[:enc_ch], t[enc_ch : 2 * enc_ch], t[2 * enc_ch :])

        def wide(v, by):
            return jnp.concatenate([paced(v[:, :width], by), paced(v[:, width:], by)], axis=1)

        def project(o):
            before, mid, after = parts[o - 1][0], parts[o][1], parts[o + 1][2]
            before = wide(before, {0: low, 8: up}.get(o))
            after = wide(after, {-1: low, 7: up}.get(o))
            second = leaky(before + mid + after).astype(bf16)
            d = dot(w3_ref[...], second).astype(bf16).astype(f32)
            for half in range(2):
                row = 2 * o + half + 8
                dmap[pl.ds(row, desc_ch, stride=33), :] = d[:, half * width : (half + 1) * width]

        part = functools.partial
        steps = [start, part(conv_first, -10, slice(6 * enc_ch, None), (0,))]
        steps += [part(conv_first, -8 + i, slice(i * enc_ch, (i + 2) * enc_ch), (16,), (32, low)) for i in range(0, 8, 2)]
        steps += [part(conv_first, 8 + i, slice(i * enc_ch, (i + 2) * enc_ch), (48,), (64, up)) for i in range(0, 8, 2)]
        steps += [part(conv_first, 24, slice(0, 2 * enc_ch), (80,))]
        steps += [part(activate, r) for r in range(-10, 26)]
        for p in range(-5, 13):
            steps.append(part(conv_second, p))
            if p - LAG >= -4:
                steps.append(part(project, p - LAG))
        steps += [part(project, p) for p in range(13 - LAG, 12)]
        return steps

    def windows(dmap, c):
        top = iota((8, width), 0) < RADIUS
        for a in range(WINDOW):
            at = c * 33 + a
            win[a, c] = dmap[pl.ds(at + RADIUS, 16), :].astype(bf16)
            rim = jnp.where(top, dmap[pl.ds(at, 8), :], dmap[pl.ds(at + 16, 8), :])
            winh[a, c] = jnp.concatenate([rim, rim], axis=0).astype(bf16)

    def both(u, v):
        uv = jnp.concatenate([u, v], axis=0)
        return uv[: u.shape[0]], uv[u.shape[0] :]

    def accumulate(state, n, left, right, c):
        mine = [both(left(i, c), left(i, c + 1)) for i in range(n)]
        mine = [[m * one_row for m in pair] for pair in mine]
        fresh = c % 8 == 0
        part = [None] * (WINDOW * n) if fresh else state["part"]
        for a in range(WINDOW):
            other = both(right(a, c), right(a, c + 1))
            for i in range(n):
                at = a * n + i
                v = mine[i][0] * other[0]
                part[at] = v if fresh else part[at] + v
                part[at] = part[at] + mine[i][1] * other[1]
        state["part"] = part
        if c % 8 == 6:
            pace["tick"] = part[0][:8].astype(f32) * (1.0 - one) + one
        if c % 8 == 6:
            total = state.get("total")
            state["total"] = part if total is None else [p + q for p, q in zip(total, part)]

    def put(cost, v, by, d, row):
        v = col_shift(v, by)
        last = WINDOW * WINDOW - 1
        for i, s in ((0, 0),) if d < last else ((0, -1), (1, 0), (2, 1)):
            moved = v if s == 0 else col_shift(v, s)
            cost[pl.ds(row * 97 + d + i, 8, stride=97), :] = moved

    def correlate(dmap, cost, sec_i, low_p, up_p, low_s, up_s):
        scale = 1.0 / math.sqrt(desc_ch)
        y = iota((8, width), 0)

        def tile_rows(state, b0, n, a):
            for i in range(n):
                v = state["total"][a * n + i].astype(f32) * scale
                by = b0 + i - RADIUS
                d = a * WINDOW + b0 + i
                first, second = v[:8], v[8:]
                if a < RADIUS:
                    first = jnp.where(y + (a - RADIUS) < 0, first * low_p, first)
                if a > RADIUS:
                    second = jnp.where(y + (8 + a - RADIUS) >= 16, second * up_p, second)
                put(cost, first, by, d, RADIUS)
                put(cost, second, by, d, RADIUS + 8)

        def halo_rows(state, q0, n, a):
            yh = jnp.where(y < RADIUS, y - RADIUS, y + 12)
            side = jnp.where(y < RADIUS, low_s, up_s) * scale
            torn = jnp.where(y < RADIUS, low_p, up_p)
            yp = yh + (a - RADIUS)
            mask = jnp.where((yp >= 0) & (yp < 16), side * torn, side)
            for i in range(n):
                v = state["total"][a * n + i].astype(f32)
                for h in range(2):
                    b = 2 * (q0 + i) + h
                    if b < WINDOW:
                        puth(cost, v[8 * h : 8 * h + 8] * mask, b - RADIUS, a * WINDOW + b)

        part = functools.partial
        steps = [part(windows, dmap, c) for c in range(desc_ch)]
        for b0 in range(0, WINDOW, 2):
            n = min(2, WINDOW - b0)
            state = {}

            def left(i, c, b0=b0):
                return own[sec_i, b0 + i, c]

            def right(a, c):
                return win[a, c]

            steps += [part(accumulate, state, n, left, right, c) for c in range(0, desc_ch, 2)]
            steps += [part(tile_rows, state, b0, n, a) for a in range(WINDOW)]
        for q0 in range(0, (WINDOW + 1) // 2, 2):
            n = min(2, (WINDOW + 1) // 2 - q0)
            state = {}

            def left(i, c, q0=q0):
                return ownh[sec_i, q0 + i, c]

            def right(a, c):
                return winh[a, c]

            steps += [part(accumulate, state, n, left, right, c) for c in range(0, desc_ch, 2)]
            steps += [part(halo_rows, state, q0, n, a) for a in range(WINDOW)]
        return steps

    def puth(cost, v, by, d):
        v = col_shift(v, by)
        last = WINDOW * WINDOW - 1
        for i, s in ((0, 0),) if d < last else ((0, -1), (1, 0), (2, 1)):
            moved = v if s == 0 else col_shift(v, s)
            cost[pl.ds(d + i, RADIUS, stride=97), :] = moved[:RADIUS]
            cost[pl.ds((RADIUS + 16) * 97 + d + i, RADIUS, stride=97), :] = moved[RADIUS:]

    def decode(cost, sec_i, slot, low_s, up_s):
        t1, t2, t3 = {}, {}, {}

        def cost_row(row):
            at = (row + RADIUS) * 97
            v = paced(cost[at : at + 96, :]).astype(bf16)
            return jnp.concatenate([stack_cols(v[:80], 1), v[80:]], axis=0)

        def join(t, row, pitch, n):
            before, after = t[row - 1][:n], t[row + 1][2 * pitch : 2 * pitch + n]
            if n % 8:
                return before * one + t[row][pitch : pitch + n] + after * one
            return paced(before) + t[row][pitch : pitch + n] + paced(after)

        def hidden(t, row):
            v = leaky(join(t, row, enc_ch, enc_ch))
            if row < 0:
                v = v * low_s
            if row >= 16:
                v = v * up_s
            return stack_cols(v, 1)

        def multiply(t, weights, row, rows):
            out = dot(weights, jnp.concatenate(rows, axis=1))
            t[row], t[row + 1] = out[:, :width], out[:, width:]

        def first(p):
            multiply(t1, d1c[...], 2 * p, [cost_row(2 * p), cost_row(2 * p + 1)])

        def second(p):
            multiply(t2, d2c[...], 2 * p, [hidden(t1, 2 * p), hidden(t1, 2 * p + 1)])

        def third(p):
            rows = [hidden(t2, 2 * p - 1), hidden(t2, 2 * p)]
            multiply(t3, d3c[...].astype(bf16), 2 * p - 1, rows)
            for row in (2 * p - 2, 2 * p - 1):
                if 0 <= row < 16:
                    v = join(t3, row, 8, 2)
                    for o in range(2):
                        flow_ref[sec_i, slot, o, row : row + 1, :] = v[o : o + 1, :]

        part = functools.partial
        return (
            [part(first, p) for p in range(-2, 10)]
            + [part(second, p) for p in range(-1, 9)]
            + [part(third, p) for p in range(9)]
        )

    def run(*lists):
        keyed = [
            ((k + 0.5) / len(steps), n, k, f) for n, steps in enumerate(lists) for k, f in enumerate(steps)
        ]
        pace.clear()
        for _, _, _, f in sorted(keyed, key=lambda e: e[:3]):
            f()
        pace.clear()

    def section(sec_i, carry):
        mine = sec * here + sec_i
        run(encode(dmap_a, sec_i, link(mine, tile - 1), link(mine, tile)))

        def keep_own(c, carry):
            tile_rows = dmap_a[pl.ds(c * 33 + 8, 16), :].astype(bf16)
            top = iota((8, width), 0) < RADIUS
            rim = jnp.where(top, dmap_a[pl.ds(c * 33 + 4, 8), :], dmap_a[pl.ds(c * 33 + 20, 8), :])
            desc_ref[sec_i, c] = tile_rows

            def moved(v, b):
                by = (b - RADIUS) % width
                return pltpu.roll(v, by, axis=1) if by else v

            for b in range(WINDOW):
                own[sec_i, b, c] = moved(tile_rows, b)
            for h in range((WINDOW + 1) // 2):
                pair_rows = [moved(rim, 2 * h), moved(rim, min(2 * h + 1, WINDOW - 1))]
                ownh[sec_i, h, c] = jnp.concatenate(pair_rows, axis=0).astype(bf16)
            return carry

        return lax.fori_loop(0, desc_ch, keep_own, carry, unroll=4)

    lax.fori_loop(0, here, section, 0)

    n_slot = len(OFFSETS)
    n_pair = here * n_slot

    def pair_of(i):
        i = jnp.clip(i, 0, n_pair - 1)
        sec_i, slot = i // n_slot, i % n_slot
        mine = sec * here + sec_i
        other = partners_ref[sec_i, slot]
        dev = other // here
        near_a = (dev // 2) == ((sec // 2) ^ 1)
        block = jnp.where(dev // 2 == sec // 2, 0, jnp.where(near_a, 1, 2))
        twin = jnp.where(dev % 2 == sec % 2, 0, 1)
        cand = (block * 2 + twin) * here + other % here
        links = (link(other, tile - 1), link(other, tile), link(mine, tile - 1), link(mine, tile))
        return sec_i, slot, cand, links

    def encode_pair(i, dmap):
        _, _, cand, links = pair_of(i)
        return encode(dmap, cand, links[0], links[1])

    def decode_pair(i, cost):
        sec_i, slot, _, links = pair_of(i)
        return decode(cost, sec_i, slot, links[2], links[3])

    def phase(i, dmap, next_dmap, cost, last_cost):
        sec_i, _, _, links = pair_of(i)
        run(
            correlate(dmap, cost, sec_i, *links),
            decode_pair(i - 1, last_cost) + encode_pair(i + 1, next_dmap),
        )

    run(encode_pair(0, dmap_a))

    def two(k, carry):
        phase(2 * k, dmap_a, dmap_b, cost_a, cost_b)
        phase(2 * k + 1, dmap_b, dmap_a, cost_b, cost_a)
        return carry

    assert n_pair % 2 == 0
    lax.fori_loop(0, n_pair // 2, two, 0)
    run(decode_pair(n_pair - 1, cost_b))


def swap(x, axis, first, stride=1):
    size = lax.axis_size(axis)
    route = []
    for i in range(first * stride, size - stride):
        if (i // stride - first) % 2 == 0:
            route += [(i, i + stride), (i + stride, i)]
    return lax.ppermute(x, axis, route)


def shards(
    images, seam_links, partners, enc_first, enc_second, enc_third, dec_first, dec_second, dec_third
):
    here, height, in_width = images.shape
    assert here * 2 >= max(OFFSETS) and lax.axis_size("sec") % 2 == 0
    meta = jnp.stack([lax.axis_index("sec"), lax.axis_index("tile")]).astype(jnp.int32)
    near = jnp.concatenate([images, swap(images, "sec", 0)], axis=0)
    cands = jnp.concatenate([near, swap(near, "sec", 0, 2), swap(near, "sec", 1, 2)], axis=0)
    ha = swap(cands, "tile", 0)
    hb = swap(cands, "tile", 1)

    def taps(w):
        return jnp.transpose(w, (2, 3, 0, 1)).reshape((-1,) + w.shape[:2])

    w1 = jnp.transpose(enc_first, (1, 2, 3, 0)).reshape(9, -1)
    w3 = enc_third[:, :, 0, 0]
    enc_ch = enc_first.shape[0]
    desc_ch = enc_third.shape[0]
    rows, width = height // 2, in_width // 2
    smem = pl.BlockSpec(memory_space=pltpu.SMEM)
    vmem = pl.BlockSpec(memory_space=pltpu.VMEM)
    return pl.pallas_call(
        body,
        in_specs=[smem] * 3 + [vmem] * 9,
        out_specs=[vmem] * 2,
        out_shape=[
            jax.ShapeDtypeStruct((here, desc_ch, rows, width), bf16),
            jax.ShapeDtypeStruct((here, len(OFFSETS), dec_third.shape[0], rows, width), f32),
        ],
        scratch_shapes=[
            pltpu.VMEM((in_width, 3 * width), bf16),
            pltpu.VMEM((8 * enc_ch, 128), bf16),
            pltpu.VMEM((3 * enc_ch, 3 * enc_ch), bf16),
            pltpu.VMEM((3 * enc_ch, 256), bf16),
            pltpu.VMEM((3 * enc_ch, 3 * enc_ch), bf16),
            pltpu.VMEM((24, 3 * enc_ch), f32),
            pltpu.VMEM((desc_ch * 33, width), f32),
            pltpu.VMEM((desc_ch * 33, width), f32),
            pltpu.VMEM((here, WINDOW, desc_ch, rows, width), bf16),
            pltpu.VMEM((here, (WINDOW + 1) // 2, desc_ch, rows, width), bf16),
            pltpu.VMEM((WINDOW, desc_ch, rows, width), bf16),
            pltpu.VMEM((WINDOW, desc_ch, rows, width), bf16),
            pltpu.VMEM((24 * 97, width), f32),
            pltpu.VMEM((24 * 97, width), f32),
        ],
        compiler_params=pltpu.CompilerParams(vmem_limit_bytes=48 * 1024 * 1024),
    )(meta, seam_links, partners, cands, ha, hb, w1, taps(enc_second), w3, taps(dec_first),
      taps(dec_second), taps(dec_third))


def solution(mesh):
    return jax.shard_map(
        shards,
        mesh=mesh,
        in_specs=(P("sec", "tile", None), P(), P("sec", None), P(), P(), P(), P(), P(), P()),
        out_specs=(P("sec", None, "tile", None), P("sec", None, None, "tile", None)),
        check_vma=False,
    )
```

time: 79.6 us -> 51.8 us (0.65)
  Pallas kernels: 59.7 us -> 31.9 us
    pallas_call x1, Pallas kernels: 59.7 us -> 31.9 us  [shards(): pl.pallas_call(body, in_specs=[smem] * 3 + [vmem] * 9, out_specs=[vmem] *...]
  transfers between devices with their start and end apart: 5 -> 5, of which waited for: 3 -> 3; matrix products, arithmetic and copies ran while one was open for 1% -> 2% of each run, Pallas kernels for 0% -> 0%
where the time goes in v1:
time: 51.8 us; the launch traced here: 51.6 us
  Pallas kernels  31.9 us (62%)
  starting transfers between devices  10.9 us (21%)
  waiting for transfers between devices  7 us (14%)
  local copies, waits for them, and re-layouts  0.98 us (2%)
  between operations  0.75 us (1%)
    pallas_call x1, Pallas kernels, shards(): pl.pallas_call(body, in_specs=[smem] * 3 + [vmem] * 9, out_specs=[vmem] *...  31.9 us
    ppermute x5, starting transfers between devices, swap(): return lax.ppermute(x, axis, route)  10.9 us
    ppermute x5, waiting for transfers between devices, swap(): return lax.ppermute(x, axis, route)  7 us
  transfers between devices with their start and end apart: 5, of which 3 were waited for; matrix products, arithmetic and copies ran while one was open for 2% of the time, Pallas kernels for 0%

profile of v1, /device:TPU:17, one launch (start us, length us, event | category | flops | bytes accessed | tf_op | source)
XLA Modules:
  0.0 51.6 jit_solution(17393723995388390408)
XLA Ops:
  0.6 1.3 %collective-permute-start = (bf16[2,32,256]{2,1,0:T(8,128)(2,1)}, bf16[2,32,256]{2,1,0:T(8,128)(2,1)S(1)}, u32[]{:S(2)}, u32[]{:S(2)}) collective-permute-start(bf16[2,32,256]{2,1,0:T(8,128)(2,1)} %param.9), channel_id=1, source_target_pairs={{0,4},{4,0},{8,12},{12,8},{16,20},{20,16},{24,28},{28,24},{1,5},{5... | collective-permute-start | bytes 98312 | tf_op jit(solution)/shard_map/ppermute | solution.py:420
  1.9 0.8 %constant_dynamic-update-slice_fusion.1 = (bf16[4,32,256]{2,1,0:T(8,128)(2,1)S(1)}, bf16[12,32,256]{2,1,0:T(8,128)(2,1)S(1)}) fusion(bf16[2,32,256]{2,1,0:T(8,128)(2,1)} %param.9), kind=kLoop, calls=%fused_computation.1 | loop fusion | bytes 98304
  2.8 0.9 %collective-permute-done = bf16[2,32,256]{2,1,0:T(8,128)(2,1)S(1)} collective-permute-done((bf16[2,32,256]{2,1,0:T(8,128)(2,1)}, bf16[2,32,256]{2,1,0:T(8,128)(2,1)S(1)}, u32[]{:S(2)}, u32[]{:S(2)}) %collective-permute-start) | collective-permute-done | bytes 32800 | tf_op jit(solution)/shard_map/ppermute | solution.py:420
  3.7 1.4 %collective-permute-start.1 = (bf16[4,32,256]{2,1,0:T(8,128)(2,1)S(1)}, bf16[4,32,256]{2,1,0:T(8,128)(2,1)S(1)}, u32[]{:S(2)}, u32[]{:S(2)}) collective-permute-start(bf16[4,32,256]{2,1,0:T(8,128)(2,1)S(1)} %get-tuple-element.2), channel_id=1, source_target_pairs={{0,8},{8,0},{4,12},{12,4},{16,24},{24,16},{20,28},{28,20},{1,9},{9... | collective-permute-start | bytes 196616 | tf_op jit(solution)/shard_map/ppermute | solution.py:420
  5.0 1.9 %collective-permute-start.2 = (bf16[4,32,256]{2,1,0:T(8,128)(2,1)S(1)}, bf16[4,32,256]{2,1,0:T(8,128)(2,1)S(1)}, u32[]{:S(2)}, u32[]{:S(2)}) collective-permute-start(bf16[4,32,256]{2,1,0:T(8,128)(2,1)S(1)} %get-tuple-element.2), channel_id=1, source_target_pairs={{8,16},{16,8},{12,20},{20,12},{9,17},{17,9},{13,21},{21,13},{10,18... | collective-permute-start | bytes 196616 | tf_op jit(solution)/shard_map/ppermute | solution.py:420
  7.0 0.0 collective-permute-done.1
  7.0 0.0 copy-start
  7.0 0.0 copy-start.1
  7.0 3.0 %collective-permute-done.2 = bf16[4,32,256]{2,1,0:T(8,128)(2,1)S(1)} collective-permute-done((bf16[4,32,256]{2,1,0:T(8,128)(2,1)S(1)}, bf16[4,32,256]{2,1,0:T(8,128)(2,1)S(1)}, u32[]{:S(2)}, u32[]{:S(2)}) %collective-permute-start.2) | collective-permute-done | bytes 65568 | tf_op jit(solution)/shard_map/ppermute | solution.py:420
  10.1 6.2 %collective-permute-start.4 = (bf16[12,32,256]{2,1,0:T(8,128)(2,1)S(1)}, bf16[12,32,256]{2,1,0:T(8,128)(2,1)S(1)}, u32[]{:S(2)}, u32[]{:S(2)}) collective-permute-start(bf16[12,32,256]{2,1,0:T(8,128)(2,1)S(1)} %constant_dynamic-update-slice_fusion.2.img_ref), channel_id=1, source_target_pairs={{1,2},{2,1},{5,6},{6,5},{9,10},{10,9},{13,14},{14,13},{17,18},{18,... | collective-permute-start | bytes 589832 | tf_op jit(solution)/shard_map/ppermute | solution.py:420
  16.3 0.1 collective-permute-start.3
  16.4 0.0 copy-done.6
  16.4 0.0 copy-done.7
  16.4 0.1 copy.11.links_ref
  16.5 0.1 pad_add_fusion.meta_ref
  16.6 3.1 %collective-permute-done.4.hb_ref = bf16[12,32,256]{2,1,0:T(8,128)(2,1)S(1)} collective-permute-done((bf16[12,32,256]{2,1,0:T(8,128)(2,1)S(1)}, bf16[12,32,256]{2,1,0:T(8,128)(2,1)S(1)}, u32[]{:S(2)}, u32[]{:S(2)}) %collective-permute-start.4) | collective-permute-done | bytes 196640 | tf_op jit(solution)/shard_map/ppermute | solution.py:420
  19.6 0.0 collective-permute-done.3.ha_ref
  19.6 0.0 copy-done.2
  19.7 0.0 copy-done.5
  19.7 0.0 copy-done
  19.7 0.0 copy-done.1
  19.7 0.0 copy-done.3
  19.7 0.0 copy-done.4
  19.7 31.9 %shard_map.104 = (bf16[2,32,16,128]{3,2,1,0:T(8,128)(2,1)}, f32[2,3,2,16,128]{4,3,2,1,0:T(8,128)}) custom-call(s32[2]{0:T(128)S(1)} %pad_add_fusion.meta_ref, s32[16,3]{1,0:T(8,128)S(1)} %copy.11.links_ref, s32[2,3]{1,0:T(2,128)S(1)} %copy-done.5, bf16[12,32,256]{2,1,0:T(8,128)(2,1)S(1)} %constant_dynamic-update-slice_fusion.2.img_ref, ...), custom_call_target="tpu_custom_call" | custom-call | tf_op jit(solution)/shard_map/pallas_call | solution.py:444
  (10 shorter events, 0.0 us)
Async XLA Ops:
  0.6 3.0 %collective-permute-start = (bf16[2,32,256]{2,1,0:T(8,128)(2,1)}, bf16[2,32,256]{2,1,0:T(8,128)(2,1)S(1)}, u32[]{:S(2)}, u32[]{:S(2)}) collective-permute-start(bf16[2,32,256]{2,1,0:T(8,128)(2,1)} %param.9), channel_id=1, source_target_pairs={{0,4},{4,0},{8,12},{12,8},{16,20},{20,16},{24,28},{28,24},{1,5},{5... | collective-permute-start | bytes 98312 | tf_op jit(solution)/shard_map/ppermute | solution.py:420
  1.9 17.7 %copy-start.2 = (bf16[64,64,3,3]{1,0,3,2:T(8,128)(2,1)S(1)}, bf16[64,64,3,3]{1,0,3,2:T(8,128)(2,1)}, u32[]{:S(2)}) copy-start(bf16[64,64,3,3]{1,0,3,2:T(8,128)(2,1)} %param.16) | copy-start | bytes 221188
  3.7 12.7 %copy-start.6 = (bf16[64,1,3,3]{0,3,2,1:T(4,128)(2,1)S(1)}, bf16[64,1,3,3]{0,3,2,1:T(4,128)(2,1)}, u32[]{:S(2)}) copy-start(bf16[64,1,3,3]{0,3,2,1:T(4,128)(2,1)} %param.12) | copy-start | bytes 3460
  3.7 12.7 %copy-start.7 = (s32[16,3]{0,1:T(4,128)S(1)}, s32[16,3]{0,1:T(4,128)}, u32[]{:S(2)}) copy-start(s32[16,3]{0,1:T(4,128)} %param.10) | copy-start | bytes 580
  3.7 16.0 %copy-start.5 = (s32[2,3]{1,0:T(2,128)S(1)}, s32[2,3]{1,0:T(2,128)}, u32[]{:S(2)}) copy-start(s32[2,3]{1,0:T(2,128)} %partners_ref.1) | copy-start | bytes 76
  3.7 3.3 %collective-permute-start.1 = (bf16[4,32,256]{2,1,0:T(8,128)(2,1)S(1)}, bf16[4,32,256]{2,1,0:T(8,128)(2,1)S(1)}, u32[]{:S(2)}, u32[]{:S(2)}) collective-permute-start(bf16[4,32,256]{2,1,0:T(8,128)(2,1)S(1)} %get-tuple-element.2), channel_id=1, source_target_pairs={{0,8},{8,0},{4,12},{12,4},{16,24},{24,16},{20,28},{28,20},{1,9},{9... | collective-permute-start | bytes 196616 | tf_op jit(solution)/shard_map/ppermute | solution.py:420
  5.0 5.0 %collective-permute-start.2 = (bf16[4,32,256]{2,1,0:T(8,128)(2,1)S(1)}, bf16[4,32,256]{2,1,0:T(8,128)(2,1)S(1)}, u32[]{:S(2)}, u32[]{:S(2)}) collective-permute-start(bf16[4,32,256]{2,1,0:T(8,128)(2,1)S(1)} %get-tuple-element.2), channel_id=1, source_target_pairs={{8,16},{16,8},{12,20},{20,12},{9,17},{17,9},{13,21},{21,13},{10,18... | collective-permute-start | bytes 196616 | tf_op jit(solution)/shard_map/ppermute | solution.py:420
  7.0 12.7 %copy-start = (bf16[64,64,3,3]{1,0,3,2:T(8,128)(2,1)S(1)}, bf16[64,64,3,3]{1,0,3,2:T(8,128)(2,1)}, u32[]{:S(2)}) copy-start(bf16[64,64,3,3]{1,0,3,2:T(8,128)(2,1)} %param.13) | copy-start | bytes 221188
  7.0 12.7 %copy-start.1 = (bf16[64,81,3,3]{1,0,3,2:T(8,128)(2,1)S(1)}, bf16[64,81,3,3]{1,0,3,2:T(8,128)(2,1)}, u32[]{:S(2)}) copy-start(bf16[64,81,3,3]{1,0,3,2:T(8,128)(2,1)} %param.15) | copy-start | bytes 279940
  10.1 9.6 %collective-permute-start.4 = (bf16[12,32,256]{2,1,0:T(8,128)(2,1)S(1)}, bf16[12,32,256]{2,1,0:T(8,128)(2,1)S(1)}, u32[]{:S(2)}, u32[]{:S(2)}) collective-permute-start(bf16[12,32,256]{2,1,0:T(8,128)(2,1)S(1)} %constant_dynamic-update-slice_fusion.2.img_ref), channel_id=1, source_target_pairs={{1,2},{2,1},{5,6},{6,5},{9,10},{10,9},{13,14},{14,13},{17,18},{18,... | collective-permute-start | bytes 589832 | tf_op jit(solution)/shard_map/ppermute | solution.py:420
  16.3 3.3 %collective-permute-start.3 = (bf16[12,32,256]{2,1,0:T(8,128)(2,1)S(1)}, bf16[12,32,256]{2,1,0:T(8,128)(2,1)S(1)}, u32[]{:S(2)}, u32[]{:S(2)}) collective-permute-start(bf16[12,32,256]{2,1,0:T(8,128)(2,1)S(1)} %constant_dynamic-update-slice_fusion.2.img_ref), channel_id=1, source_target_pairs={{0,1},{1,0},{2,3},{3,2},{4,5},{5,4},{6,7},{7,6},{8,9},{9,8},{10,11... | collective-permute-start | bytes 589832 | tf_op jit(solution)/shard_map/ppermute | solution.py:420
  16.5 3.2 %copy-start.3 = (bf16[32,64,1,1]{1,0,3,2:T(8,128)(2,1)S(1)}, bf16[32,64,1,1]{1,0,3,2:T(8,128)(2,1)}, u32[]{:S(2)}) copy-start(bf16[32,64,1,1]{1,0,3,2:T(8,128)(2,1)} %param.14) | copy-start | bytes 12292
  16.6 3.1 %copy-start.4 = (bf16[2,64,3,3]{1,0,3,2:T(2,128)(2,1)S(1)}, bf16[2,64,3,3]{1,0,3,2:T(2,128)(2,1)}, u32[]{:S(2)}) copy-start(bf16[2,64,3,3]{1,0,3,2:T(2,128)(2,1)} %param.17) | copy-start | bytes 6916

commit v2 on v1

--- a/solution.py
+++ b/solution.py
@@ -50,7 +50,7 @@
     meta_ref, links_ref, partners_ref, img_ref, ha_ref, hb_ref,
     w1_ref, w2_ref, w3_ref, d1_ref, d2_ref, d3_ref,
     desc_ref, flow_ref,
-    sel, w1t, w2c, d1c, d2c, d3c, dmap_a, dmap_b, own, ownh, win, winh, cost_a, cost_b,
+    sel, w1t, w2c, d1c, d2c, d3c, dmap_a, dmap_b, own, cost_a, cost_b,
 ):
     here = img_ref.shape[0] // 6
     n_seam = links_ref.shape[1]
@@ -96,7 +96,6 @@
     even = tile % 2 == 0
     one = jnp.where(tile >= 0, 1.0, 0.0).astype(f32)
     pace = {}
-    one_row = (jnp.zeros((16, width), f32) + one).astype(bf16)
 
     def paced(v, by=None):
         tick = pace.get("tick")
@@ -182,36 +181,18 @@
         steps += [part(project, p) for p in range(13 - LAG, 12)]
         return steps
 
-    def windows(dmap, c):
-        top = iota((8, width), 0) < RADIUS
+    def accumulate(state, dmap, sec_i, k, g, c):
+        mine = [own[sec_i, 3 * g + b, c * 24 + 8 * k : c * 24 + 8 * k + 8, :] * one for b in range(3)]
+        acc = state.get("acc")
+        new = []
         for a in range(WINDOW):
-            at = c * 33 + a
-            win[a, c] = dmap[pl.ds(at + RADIUS, 16), :].astype(bf16)
-            rim = jnp.where(top, dmap[pl.ds(at, 8), :], dmap[pl.ds(at + 16, 8), :])
-            winh[a, c] = jnp.concatenate([rim, rim], axis=0).astype(bf16)
-
-    def both(u, v):
-        uv = jnp.concatenate([u, v], axis=0)
-        return uv[: u.shape[0]], uv[u.shape[0] :]
-
-    def accumulate(state, n, left, right, c):
-        mine = [both(left(i, c), left(i, c + 1)) for i in range(n)]
-        mine = [[m * one_row for m in pair] for pair in mine]
-        fresh = c % 8 == 0
-        part = [None] * (WINDOW * n) if fresh else state["part"]
-        for a in range(WINDOW):
-            other = both(right(a, c), right(a, c + 1))
-            for i in range(n):
-                at = a * n + i
-                v = mine[i][0] * other[0]
-                part[at] = v if fresh else part[at] + v
-                part[at] = part[at] + mine[i][1] * other[1]
-        state["part"] = part
-        if c % 8 == 6:
-            pace["tick"] = part[0][:8].astype(f32) * (1.0 - one) + one
-        if c % 8 == 6:
-            total = state.get("total")
-            state["total"] = part if total is None else [p + q for p, q in zip(total, part)]
+            other = dmap[pl.ds(c * 33 + 8 * k + a, 8), :]
+            for b in range(3):
+                v = mine[b] * other
+                new.append(v if acc is None else acc[3 * a + b] + v)
+        state["acc"] = new
+        if c % 8 == 7:
+            pace["tick"] = new[0] * (1.0 - one) + one
 
     def put(cost, v, by, d, row):
         v = col_shift(v, by)
@@ -222,69 +203,27 @@
 
     def correlate(dmap, cost, sec_i, low_p, up_p, low_s, up_s):
         scale = 1.0 / math.sqrt(desc_ch)
-        y = iota((8, width), 0)
-
-        def tile_rows(state, b0, n, a):
-            for i in range(n):
-                v = state["total"][a * n + i].astype(f32) * scale
-                by = b0 + i - RADIUS
-                d = a * WINDOW + b0 + i
-                first, second = v[:8], v[8:]
-                if a < RADIUS:
-                    first = jnp.where(y + (a - RADIUS) < 0, first * low_p, first)
-                if a > RADIUS:
-                    second = jnp.where(y + (8 + a - RADIUS) >= 16, second * up_p, second)
-                put(cost, first, by, d, RADIUS)
-                put(cost, second, by, d, RADIUS + 8)
-
-        def halo_rows(state, q0, n, a):
-            yh = jnp.where(y < RADIUS, y - RADIUS, y + 12)
-            side = jnp.where(y < RADIUS, low_s, up_s) * scale
-            torn = jnp.where(y < RADIUS, low_p, up_p)
-            yp = yh + (a - RADIUS)
-            mask = jnp.where((yp >= 0) & (yp < 16), side * torn, side)
-            for i in range(n):
-                v = state["total"][a * n + i].astype(f32)
-                for h in range(2):
-                    b = 2 * (q0 + i) + h
-                    if b < WINDOW:
-                        puth(cost, v[8 * h : 8 * h + 8] * mask, b - RADIUS, a * WINDOW + b)
+
+        def finish(state, k, g, a):
+            y = iota((8, width), 0) + (8 * k - RADIUS)
+            yp = y + (a - RADIUS)
+            mask = jnp.where(y < 0, low_s, jnp.where(y >= 16, up_s, 1.0)) * scale
+            if k == 0:
+                mask = jnp.where((y < 0) != (yp < 0), mask * low_p, mask)
+            if k == 2:
+                mask = jnp.where((y < 16) != (yp < 16), mask * up_p, mask)
+            for b in range(3):
+                v = state["acc"][3 * a + b] * (scale if k == 1 else mask)
+                put(cost, v, 3 * g + b - RADIUS, a * WINDOW + 3 * g + b, 8 * k)
 
         part = functools.partial
-        steps = [part(windows, dmap, c) for c in range(desc_ch)]
-        for b0 in range(0, WINDOW, 2):
-            n = min(2, WINDOW - b0)
-            state = {}
-
-            def left(i, c, b0=b0):
-                return own[sec_i, b0 + i, c]
-
-            def right(a, c):
-                return win[a, c]
-
-            steps += [part(accumulate, state, n, left, right, c) for c in range(0, desc_ch, 2)]
-            steps += [part(tile_rows, state, b0, n, a) for a in range(WINDOW)]
-        for q0 in range(0, (WINDOW + 1) // 2, 2):
-            n = min(2, (WINDOW + 1) // 2 - q0)
-            state = {}
-
-            def left(i, c, q0=q0):
-                return ownh[sec_i, q0 + i, c]
-
-            def right(a, c):
-                return winh[a, c]
-
-            steps += [part(accumulate, state, n, left, right, c) for c in range(0, desc_ch, 2)]
-            steps += [part(halo_rows, state, q0, n, a) for a in range(WINDOW)]
+        steps = []
+        for k in range(3):
+            for g in range(3):
+                state = {}
+                steps += [part(accumulate, state, dmap, sec_i, k, g, c) for c in range(desc_ch)]
+                steps += [part(finish, state, k, g, a) for a in range(WINDOW)]
         return steps
-
-    def puth(cost, v, by, d):
-        v = col_shift(v, by)
-        last = WINDOW * WINDOW - 1
-        for i, s in ((0, 0),) if d < last else ((0, -1), (1, 0), (2, 1)):
-            moved = v if s == 0 else col_shift(v, s)
-            cost[pl.ds(d + i, RADIUS, stride=97), :] = moved[:RADIUS]
-            cost[pl.ds((RADIUS + 16) * 97 + d + i, RADIUS, stride=97), :] = moved[RADIUS:]
 
     def decode(cost, sec_i, slot, low_s, up_s):
         t1, t2, t3 = {}, {}, {}
@@ -348,20 +287,13 @@
         run(encode(dmap_a, sec_i, link(mine, tile - 1), link(mine, tile)))
 
         def keep_own(c, carry):
-            tile_rows = dmap_a[pl.ds(c * 33 + 8, 16), :].astype(bf16)
-            top = iota((8, width), 0) < RADIUS
-            rim = jnp.where(top, dmap_a[pl.ds(c * 33 + 4, 8), :], dmap_a[pl.ds(c * 33 + 20, 8), :])
-            desc_ref[sec_i, c] = tile_rows
-
-            def moved(v, b):
-                by = (b - RADIUS) % width
-                return pltpu.roll(v, by, axis=1) if by else v
-
-            for b in range(WINDOW):
-                own[sec_i, b, c] = moved(tile_rows, b)
-            for h in range((WINDOW + 1) // 2):
-                pair_rows = [moved(rim, 2 * h), moved(rim, min(2 * h + 1, WINDOW - 1))]
-                ownh[sec_i, h, c] = jnp.concatenate(pair_rows, axis=0).astype(bf16)
+            desc_ref[sec_i, c] = dmap_a[pl.ds(c * 33 + 8, 16), :].astype(bf16)
+            for k in range(3):
+                v = dmap_a[pl.ds(c * 33 + RADIUS + 8 * k, 8), :]
+                at = pl.multiple_of(c * 24, 8) + 8 * k
+                for b in range(WINDOW):
+                    by = (b - RADIUS) % width
+                    own[sec_i, b, pl.ds(at, 8), :] = pltpu.roll(v, by, axis=1) if by else v
             return carry
 
         return lax.fori_loop(0, desc_ch, keep_own, carry, unroll=4)
@@ -458,10 +390,7 @@
             pltpu.VMEM((24, 3 * enc_ch), f32),
             pltpu.VMEM((desc_ch * 33, width), f32),
             pltpu.VMEM((desc_ch * 33, width), f32),
-            pltpu.VMEM((here, WINDOW, desc_ch, rows, width), bf16),
-            pltpu.VMEM((here, (WINDOW + 1) // 2, desc_ch, rows, width), bf16),
-            pltpu.VMEM((WINDOW, desc_ch, rows, width), bf16),
-            pltpu.VMEM((WINDOW, desc_ch, rows, width), bf16),
+            pltpu.VMEM((here, WINDOW, desc_ch * 24, width), f32),
             pltpu.VMEM((24 * 97, width), f32),
             pltpu.VMEM((24 * 97, width), f32),
         ],

time: 51.8 us -> 62.2 us (1.20)
  Pallas kernels: 31.9 us -> 42.4 us
    pallas_call x1, Pallas kernels: 31.9 us -> 42.4 us  [shards(): pl.pallas_call(body, in_specs=[smem] * 3 + [vmem] * 9, out_specs=[vmem] *...]
where the time goes in v2:
time: 62.2 us; the launch traced here: 62.1 us
  Pallas kernels  42.4 us (68%)
  starting transfers between devices  10.9 us (18%)
  waiting for transfers between devices  7 us (11%)
  local copies, waits for them, and re-layouts  0.98 us (2%)
  between operations  0.75 us (1%)
    pallas_call x1, Pallas kernels, shards(): pl.pallas_call(body, in_specs=[smem] * 3 + [vmem] * 9, out_specs=[vmem] *...  42.4 us
    ppermute x5, starting transfers between devices, swap(): return lax.ppermute(x, axis, route)  10.9 us
    ppermute x5, waiting for transfers between devices, swap(): return lax.ppermute(x, axis, route)  7 us
  transfers between devices with their start and end apart: 5, of which 3 were waited for; matrix products, arithmetic and copies ran while one was open for 2% of the time, Pallas kernels for 0%

profile of v2, /device:TPU:17, one launch (start us, length us, event | category | flops | bytes accessed | tf_op | source)
XLA Modules:
  0.0 62.1 jit_solution(10092289407398704736)
XLA Ops:
  0.6 1.3 %collective-permute-start = (bf16[2,32,256]{2,1,0:T(8,128)(2,1)}, bf16[2,32,256]{2,1,0:T(8,128)(2,1)S(1)}, u32[]{:S(2)}, u32[]{:S(2)}) collective-permute-start(bf16[2,32,256]{2,1,0:T(8,128)(2,1)} %param.9), channel_id=1, source_target_pairs={{0,4},{4,0},{8,12},{12,8},{16,20},{20,16},{24,28},{28,24},{1,5},{5... | collective-permute-start | bytes 98312 | tf_op jit(solution)/shard_map/ppermute | solution.py:352
  1.9 0.8 %constant_dynamic-update-slice_fusion.1 = (bf16[4,32,256]{2,1,0:T(8,128)(2,1)S(1)}, bf16[12,32,256]{2,1,0:T(8,128)(2,1)S(1)}) fusion(bf16[2,32,256]{2,1,0:T(8,128)(2,1)} %param.9), kind=kLoop, calls=%fused_computation.1 | loop fusion | bytes 98304
  2.8 0.9 %collective-permute-done = bf16[2,32,256]{2,1,0:T(8,128)(2,1)S(1)} collective-permute-done((bf16[2,32,256]{2,1,0:T(8,128)(2,1)}, bf16[2,32,256]{2,1,0:T(8,128)(2,1)S(1)}, u32[]{:S(2)}, u32[]{:S(2)}) %collective-permute-start) | collective-permute-done | bytes 32800 | tf_op jit(solution)/shard_map/ppermute | solution.py:352
  3.7 1.4 %collective-permute-start.1 = (bf16[4,32,256]{2,1,0:T(8,128)(2,1)S(1)}, bf16[4,32,256]{2,1,0:T(8,128)(2,1)S(1)}, u32[]{:S(2)}, u32[]{:S(2)}) collective-permute-start(bf16[4,32,256]{2,1,0:T(8,128)(2,1)S(1)} %get-tuple-element.2), channel_id=1, source_target_pairs={{0,8},{8,0},{4,12},{12,4},{16,24},{24,16},{20,28},{28,20},{1,9},{9... | collective-permute-start | bytes 196616 | tf_op jit(solution)/shard_map/ppermute | solution.py:352
  5.0 1.9 %collective-permute-start.2 = (bf16[4,32,256]{2,1,0:T(8,128)(2,1)S(1)}, bf16[4,32,256]{2,1,0:T(8,128)(2,1)S(1)}, u32[]{:S(2)}, u32[]{:S(2)}) collective-permute-start(bf16[4,32,256]{2,1,0:T(8,128)(2,1)S(1)} %get-tuple-element.2), channel_id=1, source_target_pairs={{8,16},{16,8},{12,20},{20,12},{9,17},{17,9},{13,21},{21,13},{10,18... | collective-permute-start | bytes 196616 | tf_op jit(solution)/shard_map/ppermute | solution.py:352
  7.0 0.0 collective-permute-done.1
  7.0 0.0 copy-start
  7.0 0.0 copy-start.1
  7.0 3.0 %collective-permute-done.2 = bf16[4,32,256]{2,1,0:T(8,128)(2,1)S(1)} collective-permute-done((bf16[4,32,256]{2,1,0:T(8,128)(2,1)S(1)}, bf16[4,32,256]{2,1,0:T(8,128)(2,1)S(1)}, u32[]{:S(2)}, u32[]{:S(2)}) %collective-permute-start.2) | collective-permute-done | bytes 65568 | tf_op jit(solution)/shard_map/ppermute | solution.py:352
  10.1 6.2 %collective-permute-start.4 = (bf16[12,32,256]{2,1,0:T(8,128)(2,1)S(1)}, bf16[12,32,256]{2,1,0:T(8,128)(2,1)S(1)}, u32[]{:S(2)}, u32[]{:S(2)}) collective-permute-start(bf16[12,32,256]{2,1,0:T(8,128)(2,1)S(1)} %constant_dynamic-update-slice_fusion.2.img_ref), channel_id=1, source_target_pairs={{1,2},{2,1},{5,6},{6,5},{9,10},{10,9},{13,14},{14,13},{17,18},{18,... | collective-permute-start | bytes 589832 | tf_op jit(solution)/shard_map/ppermute | solution.py:352
  16.3 0.1 collective-permute-start.3
  16.4 0.0 copy-done.6
  16.4 0.0 copy-done.7
  16.4 0.1 copy.11.links_ref
  16.5 0.1 pad_add_fusion.meta_ref
  16.6 3.1 %collective-permute-done.4.hb_ref = bf16[12,32,256]{2,1,0:T(8,128)(2,1)S(1)} collective-permute-done((bf16[12,32,256]{2,1,0:T(8,128)(2,1)S(1)}, bf16[12,32,256]{2,1,0:T(8,128)(2,1)S(1)}, u32[]{:S(2)}, u32[]{:S(2)}) %collective-permute-start.4) | collective-permute-done | bytes 196640 | tf_op jit(solution)/shard_map/ppermute | solution.py:352
  19.6 0.0 collective-permute-done.3.ha_ref
  19.6 0.0 copy-done.2
  19.7 0.0 copy-done.5
  19.7 0.0 copy-done
  19.7 0.0 copy-done.1
  19.7 0.0 copy-done.3
  19.7 0.0 copy-done.4
  19.7 42.4 %shard_map.104 = (bf16[2,32,16,128]{3,2,1,0:T(8,128)(2,1)}, f32[2,3,2,16,128]{4,3,2,1,0:T(8,128)}) custom-call(s32[2]{0:T(128)S(1)} %pad_add_fusion.meta_ref, s32[16,3]{1,0:T(8,128)S(1)} %copy.11.links_ref, s32[2,3]{1,0:T(2,128)S(1)} %copy-done.5, bf16[12,32,256]{2,1,0:T(8,128)(2,1)S(1)} %constant_dynamic-update-slice_fusion.2.img_ref, ...), custom_call_target="tpu_custom_call" | custom-call | tf_op jit(solution)/shard_map/pallas_call | solution.py:376
  (10 shorter events, 0.0 us)
Async XLA Ops:
  0.6 3.0 %collective-permute-start = (bf16[2,32,256]{2,1,0:T(8,128)(2,1)}, bf16[2,32,256]{2,1,0:T(8,128)(2,1)S(1)}, u32[]{:S(2)}, u32[]{:S(2)}) collective-permute-start(bf16[2,32,256]{2,1,0:T(8,128)(2,1)} %param.9), channel_id=1, source_target_pairs={{0,4},{4,0},{8,12},{12,8},{16,20},{20,16},{24,28},{28,24},{1,5},{5... | collective-permute-start | bytes 98312 | tf_op jit(solution)/shard_map/ppermute | solution.py:352
  1.9 17.7 %copy-start.2 = (bf16[64,64,3,3]{1,0,3,2:T(8,128)(2,1)S(1)}, bf16[64,64,3,3]{1,0,3,2:T(8,128)(2,1)}, u32[]{:S(2)}) copy-start(bf16[64,64,3,3]{1,0,3,2:T(8,128)(2,1)} %param.16) | copy-start | bytes 221188
  3.7 12.7 %copy-start.6 = (bf16[64,1,3,3]{0,3,2,1:T(4,128)(2,1)S(1)}, bf16[64,1,3,3]{0,3,2,1:T(4,128)(2,1)}, u32[]{:S(2)}) copy-start(bf16[64,1,3,3]{0,3,2,1:T(4,128)(2,1)} %param.12) | copy-start | bytes 3460
  3.7 12.7 %copy-start.7 = (s32[16,3]{0,1:T(4,128)S(1)}, s32[16,3]{0,1:T(4,128)}, u32[]{:S(2)}) copy-start(s32[16,3]{0,1:T(4,128)} %param.10) | copy-start | bytes 580
  3.7 16.0 %copy-start.5 = (s32[2,3]{1,0:T(2,128)S(1)}, s32[2,3]{1,0:T(2,128)}, u32[]{:S(2)}) copy-start(s32[2,3]{1,0:T(2,128)} %partners_ref.1) | copy-start | bytes 76
  3.7 3.3 %collective-permute-start.1 = (bf16[4,32,256]{2,1,0:T(8,128)(2,1)S(1)}, bf16[4,32,256]{2,1,0:T(8,128)(2,1)S(1)}, u32[]{:S(2)}, u32[]{:S(2)}) collective-permute-start(bf16[4,32,256]{2,1,0:T(8,128)(2,1)S(1)} %get-tuple-element.2), channel_id=1, source_target_pairs={{0,8},{8,0},{4,12},{12,4},{16,24},{24,16},{20,28},{28,20},{1,9},{9... | collective-permute-start | bytes 196616 | tf_op jit(solution)/shard_map/ppermute | solution.py:352
  5.0 5.0 %collective-permute-start.2 = (bf16[4,32,256]{2,1,0:T(8,128)(2,1)S(1)}, bf16[4,32,256]{2,1,0:T(8,128)(2,1)S(1)}, u32[]{:S(2)}, u32[]{:S(2)}) collective-permute-start(bf16[4,32,256]{2,1,0:T(8,128)(2,1)S(1)} %get-tuple-element.2), channel_id=1, source_target_pairs={{8,16},{16,8},{12,20},{20,12},{9,17},{17,9},{13,21},{21,13},{10,18... | collective-permute-start | bytes 196616 | tf_op jit(solution)/shard_map/ppermute | solution.py:352
  7.0 12.7 %copy-start = (bf16[64,64,3,3]{1,0,3,2:T(8,128)(2,1)S(1)}, bf16[64,64,3,3]{1,0,3,2:T(8,128)(2,1)}, u32[]{:S(2)}) copy-start(bf16[64,64,3,3]{1,0,3,2:T(8,128)(2,1)} %param.13) | copy-start | bytes 221188
  7.0 12.7 %copy-start.1 = (bf16[64,81,3,3]{1,0,3,2:T(8,128)(2,1)S(1)}, bf16[64,81,3,3]{1,0,3,2:T(8,128)(2,1)}, u32[]{:S(2)}) copy-start(bf16[64,81,3,3]{1,0,3,2:T(8,128)(2,1)} %param.15) | copy-start | bytes 279940
  10.1 9.6 %collective-permute-start.4 = (bf16[12,32,256]{2,1,0:T(8,128)(2,1)S(1)}, bf16[12,32,256]{2,1,0:T(8,128)(2,1)S(1)}, u32[]{:S(2)}, u32[]{:S(2)}) collective-permute-start(bf16[12,32,256]{2,1,0:T(8,128)(2,1)S(1)} %constant_dynamic-update-slice_fusion.2.img_ref), channel_id=1, source_target_pairs={{1,2},{2,1},{5,6},{6,5},{9,10},{10,9},{13,14},{14,13},{17,18},{18,... | collective-permute-start | bytes 589832 | tf_op jit(solution)/shard_map/ppermute | solution.py:352
  16.3 3.3 %collective-permute-start.3 = (bf16[12,32,256]{2,1,0:T(8,128)(2,1)S(1)}, bf16[12,32,256]{2,1,0:T(8,128)(2,1)S(1)}, u32[]{:S(2)}, u32[]{:S(2)}) collective-permute-start(bf16[12,32,256]{2,1,0:T(8,128)(2,1)S(1)} %constant_dynamic-update-slice_fusion.2.img_ref), channel_id=1, source_target_pairs={{0,1},{1,0},{2,3},{3,2},{4,5},{5,4},{6,7},{7,6},{8,9},{9,8},{10,11... | collective-permute-start | bytes 589832 | tf_op jit(solution)/shard_map/ppermute | solution.py:352
  16.5 3.2 %copy-start.3 = (bf16[32,64,1,1]{1,0,3,2:T(8,128)(2,1)S(1)}, bf16[32,64,1,1]{1,0,3,2:T(8,128)(2,1)}, u32[]{:S(2)}) copy-start(bf16[32,64,1,1]{1,0,3,2:T(8,128)(2,1)} %param.14) | copy-start | bytes 12292
  16.6 3.1 %copy-start.4 = (bf16[2,64,3,3]{1,0,3,2:T(2,128)(2,1)S(1)}, bf16[2,64,3,3]{1,0,3,2:T(2,128)(2,1)}, u32[]{:S(2)}) copy-start(bf16[2,64,3,3]{1,0,3,2:T(2,128)(2,1)} %param.17) | copy-start | bytes 6916

commit v3 on v2

--- a/solution.py
+++ b/solution.py
@@ -181,17 +181,17 @@
         steps += [part(project, p) for p in range(13 - LAG, 12)]
         return steps
 
-    def accumulate(state, dmap, sec_i, k, g, c):
-        mine = [own[sec_i, 3 * g + b, c * 24 + 8 * k : c * 24 + 8 * k + 8, :] * one for b in range(3)]
+    def accumulate(state, dmap, sec_i, k, b0, n, c):
+        mine = [own[sec_i, b0 + b, c * 24 + 8 * k : c * 24 + 8 * k + 8, :] * one for b in range(n)]
         acc = state.get("acc")
         new = []
         for a in range(WINDOW):
             other = dmap[pl.ds(c * 33 + 8 * k + a, 8), :]
-            for b in range(3):
+            for b in range(n):
                 v = mine[b] * other
-                new.append(v if acc is None else acc[3 * a + b] + v)
+                new.append(v if acc is None else acc[n * a + b] + v)
         state["acc"] = new
-        if c % 8 == 7:
+        if c % 16 == 15:
             pace["tick"] = new[0] * (1.0 - one) + one
 
     def put(cost, v, by, d, row):
@@ -204,7 +204,7 @@
     def correlate(dmap, cost, sec_i, low_p, up_p, low_s, up_s):
         scale = 1.0 / math.sqrt(desc_ch)
 
-        def finish(state, k, g, a):
+        def finish(state, k, b0, n, a):
             y = iota((8, width), 0) + (8 * k - RADIUS)
             yp = y + (a - RADIUS)
             mask = jnp.where(y < 0, low_s, jnp.where(y >= 16, up_s, 1.0)) * scale
@@ -212,17 +212,18 @@
                 mask = jnp.where((y < 0) != (yp < 0), mask * low_p, mask)
             if k == 2:
                 mask = jnp.where((y < 16) != (yp < 16), mask * up_p, mask)
-            for b in range(3):
-                v = state["acc"][3 * a + b] * (scale if k == 1 else mask)
-                put(cost, v, 3 * g + b - RADIUS, a * WINDOW + 3 * g + b, 8 * k)
+            for b in range(n):
+                v = state["acc"][n * a + b] * (scale if k == 1 else mask)
+                put(cost, v, b0 + b - RADIUS, a * WINDOW + b0 + b, 8 * k)
 
         part = functools.partial
         steps = []
         for k in range(3):
-            for g in range(3):
+            for b0 in range(WINDOW):
+                n = 1
                 state = {}
-                steps += [part(accumulate, state, dmap, sec_i, k, g, c) for c in range(desc_ch)]
-                steps += [part(finish, state, k, g, a) for a in range(WINDOW)]
+                steps += [part(accumulate, state, dmap, sec_i, k, b0, n, c) for c in range(desc_ch)]
+                steps += [part(finish, state, k, b0, n, a) for a in range(WINDOW)]
         return steps
 
     def decode(cost, sec_i, slot, low_s, up_s):
@@ -296,7 +297,7 @@
                     own[sec_i, b, pl.ds(at, 8), :] = pltpu.roll(v, by, axis=1) if by else v
             return carry
 
-        return lax.fori_loop(0, desc_ch, keep_own, carry, unroll=4)
+        return lax.fori_loop(0, desc_ch, keep_own, carry, unroll=8)
 
     lax.fori_loop(0, here, section, 0)
 

time: 62.2 us -> 60.6 us (0.974)
  Pallas kernels: 42.4 us -> 40.7 us
    pallas_call x1, Pallas kernels: 42.4 us -> 40.7 us  [shards(): pl.pallas_call(body, in_specs=[smem] * 3 + [vmem] * 9, out_specs=[vmem] *...]
where the time goes in v3:
time: 60.6 us; the launch traced here: 60.4 us
  Pallas kernels  40.7 us (67%)
  starting transfers between devices  10.9 us (18%)
  waiting for transfers between devices  7 us (12%)
  local copies, waits for them, and re-layouts  0.98 us (2%)
  between operations  0.75 us (1%)
    pallas_call x1, Pallas kernels, shards(): pl.pallas_call(body, in_specs=[smem] * 3 + [vmem] * 9, out_specs=[vmem] *...  40.7 us
    ppermute x5, starting transfers between devices, swap(): return lax.ppermute(x, axis, route)  10.9 us
    ppermute x5, waiting for transfers between devices, swap(): return lax.ppermute(x, axis, route)  7 us
  transfers between devices with their start and end apart: 5, of which 3 were waited for; matrix products, arithmetic and copies ran while one was open for 2% of the time, Pallas kernels for 0%

profile of v3, /device:TPU:17, one launch (start us, length us, event | category | flops | bytes accessed | tf_op | source)
XLA Modules:
  0.0 60.4 jit_solution(656173272253105917)
XLA Ops:
  0.6 1.3 %collective-permute-start = (bf16[2,32,256]{2,1,0:T(8,128)(2,1)}, bf16[2,32,256]{2,1,0:T(8,128)(2,1)S(1)}, u32[]{:S(2)}, u32[]{:S(2)}) collective-permute-start(bf16[2,32,256]{2,1,0:T(8,128)(2,1)} %param.9), channel_id=1, source_target_pairs={{0,4},{4,0},{8,12},{12,8},{16,20},{20,16},{24,28},{28,24},{1,5},{5... | collective-permute-start | bytes 98312 | tf_op jit(solution)/shard_map/ppermute | solution.py:353
  1.9 0.8 %constant_dynamic-update-slice_fusion.1 = (bf16[4,32,256]{2,1,0:T(8,128)(2,1)S(1)}, bf16[12,32,256]{2,1,0:T(8,128)(2,1)S(1)}) fusion(bf16[2,32,256]{2,1,0:T(8,128)(2,1)} %param.9), kind=kLoop, calls=%fused_computation.1 | loop fusion | bytes 98304
  2.8 0.9 %collective-permute-done = bf16[2,32,256]{2,1,0:T(8,128)(2,1)S(1)} collective-permute-done((bf16[2,32,256]{2,1,0:T(8,128)(2,1)}, bf16[2,32,256]{2,1,0:T(8,128)(2,1)S(1)}, u32[]{:S(2)}, u32[]{:S(2)}) %collective-permute-start) | collective-permute-done | bytes 32800 | tf_op jit(solution)/shard_map/ppermute | solution.py:353
  3.7 1.4 %collective-permute-start.1 = (bf16[4,32,256]{2,1,0:T(8,128)(2,1)S(1)}, bf16[4,32,256]{2,1,0:T(8,128)(2,1)S(1)}, u32[]{:S(2)}, u32[]{:S(2)}) collective-permute-start(bf16[4,32,256]{2,1,0:T(8,128)(2,1)S(1)} %get-tuple-element.2), channel_id=1, source_target_pairs={{0,8},{8,0},{4,12},{12,4},{16,24},{24,16},{20,28},{28,20},{1,9},{9... | collective-permute-start | bytes 196616 | tf_op jit(solution)/shard_map/ppermute | solution.py:353
  5.0 1.9 %collective-permute-start.2 = (bf16[4,32,256]{2,1,0:T(8,128)(2,1)S(1)}, bf16[4,32,256]{2,1,0:T(8,128)(2,1)S(1)}, u32[]{:S(2)}, u32[]{:S(2)}) collective-permute-start(bf16[4,32,256]{2,1,0:T(8,128)(2,1)S(1)} %get-tuple-element.2), channel_id=1, source_target_pairs={{8,16},{16,8},{12,20},{20,12},{9,17},{17,9},{13,21},{21,13},{10,18... | collective-permute-start | bytes 196616 | tf_op jit(solution)/shard_map/ppermute | solution.py:353
  7.0 0.0 collective-permute-done.1
  7.0 0.0 copy-start
  7.0 0.0 copy-start.1
  7.0 3.0 %collective-permute-done.2 = bf16[4,32,256]{2,1,0:T(8,128)(2,1)S(1)} collective-permute-done((bf16[4,32,256]{2,1,0:T(8,128)(2,1)S(1)}, bf16[4,32,256]{2,1,0:T(8,128)(2,1)S(1)}, u32[]{:S(2)}, u32[]{:S(2)}) %collective-permute-start.2) | collective-permute-done | bytes 65568 | tf_op jit(solution)/shard_map/ppermute | solution.py:353
  10.1 6.2 %collective-permute-start.4 = (bf16[12,32,256]{2,1,0:T(8,128)(2,1)S(1)}, bf16[12,32,256]{2,1,0:T(8,128)(2,1)S(1)}, u32[]{:S(2)}, u32[]{:S(2)}) collective-permute-start(bf16[12,32,256]{2,1,0:T(8,128)(2,1)S(1)} %constant_dynamic-update-slice_fusion.2.img_ref), channel_id=1, source_target_pairs={{1,2},{2,1},{5,6},{6,5},{9,10},{10,9},{13,14},{14,13},{17,18},{18,... | collective-permute-start | bytes 589832 | tf_op jit(solution)/shard_map/ppermute | solution.py:353
  16.3 0.1 collective-permute-start.3
  16.4 0.0 copy-done.6
  16.4 0.0 copy-done.7
  16.4 0.1 copy.11.links_ref
  16.5 0.1 pad_add_fusion.meta_ref
  16.6 3.1 %collective-permute-done.4.hb_ref = bf16[12,32,256]{2,1,0:T(8,128)(2,1)S(1)} collective-permute-done((bf16[12,32,256]{2,1,0:T(8,128)(2,1)S(1)}, bf16[12,32,256]{2,1,0:T(8,128)(2,1)S(1)}, u32[]{:S(2)}, u32[]{:S(2)}) %collective-permute-start.4) | collective-permute-done | bytes 196640 | tf_op jit(solution)/shard_map/ppermute | solution.py:353
  19.6 0.0 collective-permute-done.3.ha_ref
  19.6 0.0 copy-done.2
  19.7 0.0 copy-done.5
  19.7 0.0 copy-done
  19.7 0.0 copy-done.1
  19.7 0.0 copy-done.3
  19.7 0.0 copy-done.4
  19.7 40.7 %shard_map.104 = (bf16[2,32,16,128]{3,2,1,0:T(8,128)(2,1)}, f32[2,3,2,16,128]{4,3,2,1,0:T(8,128)}) custom-call(s32[2]{0:T(128)S(1)} %pad_add_fusion.meta_ref, s32[16,3]{1,0:T(8,128)S(1)} %copy.11.links_ref, s32[2,3]{1,0:T(2,128)S(1)} %copy-done.5, bf16[12,32,256]{2,1,0:T(8,128)(2,1)S(1)} %constant_dynamic-update-slice_fusion.2.img_ref, ...), custom_call_target="tpu_custom_call" | custom-call | tf_op jit(solution)/shard_map/pallas_call | solution.py:377
  (10 shorter events, 0.0 us)
Async XLA Ops:
  0.6 3.0 %collective-permute-start = (bf16[2,32,256]{2,1,0:T(8,128)(2,1)}, bf16[2,32,256]{2,1,0:T(8,128)(2,1)S(1)}, u32[]{:S(2)}, u32[]{:S(2)}) collective-permute-start(bf16[2,32,256]{2,1,0:T(8,128)(2,1)} %param.9), channel_id=1, source_target_pairs={{0,4},{4,0},{8,12},{12,8},{16,20},{20,16},{24,28},{28,24},{1,5},{5... | collective-permute-start | bytes 98312 | tf_op jit(solution)/shard_map/ppermute | solution.py:353
  1.9 17.7 %copy-start.2 = (bf16[64,64,3,3]{1,0,3,2:T(8,128)(2,1)S(1)}, bf16[64,64,3,3]{1,0,3,2:T(8,128)(2,1)}, u32[]{:S(2)}) copy-start(bf16[64,64,3,3]{1,0,3,2:T(8,128)(2,1)} %param.16) | copy-start | bytes 221188
  3.7 12.7 %copy-start.6 = (bf16[64,1,3,3]{0,3,2,1:T(4,128)(2,1)S(1)}, bf16[64,1,3,3]{0,3,2,1:T(4,128)(2,1)}, u32[]{:S(2)}) copy-start(bf16[64,1,3,3]{0,3,2,1:T(4,128)(2,1)} %param.12) | copy-start | bytes 3460
  3.7 12.7 %copy-start.7 = (s32[16,3]{0,1:T(4,128)S(1)}, s32[16,3]{0,1:T(4,128)}, u32[]{:S(2)}) copy-start(s32[16,3]{0,1:T(4,128)} %param.10) | copy-start | bytes 580
  3.7 16.0 %copy-start.5 = (s32[2,3]{1,0:T(2,128)S(1)}, s32[2,3]{1,0:T(2,128)}, u32[]{:S(2)}) copy-start(s32[2,3]{1,0:T(2,128)} %partners_ref.1) | copy-start | bytes 76
  3.7 3.3 %collective-permute-start.1 = (bf16[4,32,256]{2,1,0:T(8,128)(2,1)S(1)}, bf16[4,32,256]{2,1,0:T(8,128)(2,1)S(1)}, u32[]{:S(2)}, u32[]{:S(2)}) collective-permute-start(bf16[4,32,256]{2,1,0:T(8,128)(2,1)S(1)} %get-tuple-element.2), channel_id=1, source_target_pairs={{0,8},{8,0},{4,12},{12,4},{16,24},{24,16},{20,28},{28,20},{1,9},{9... | collective-permute-start | bytes 196616 | tf_op jit(solution)/shard_map/ppermute | solution.py:353
  5.0 5.0 %collective-permute-start.2 = (bf16[4,32,256]{2,1,0:T(8,128)(2,1)S(1)}, bf16[4,32,256]{2,1,0:T(8,128)(2,1)S(1)}, u32[]{:S(2)}, u32[]{:S(2)}) collective-permute-start(bf16[4,32,256]{2,1,0:T(8,128)(2,1)S(1)} %get-tuple-element.2), channel_id=1, source_target_pairs={{8,16},{16,8},{12,20},{20,12},{9,17},{17,9},{13,21},{21,13},{10,18... | collective-permute-start | bytes 196616 | tf_op jit(solution)/shard_map/ppermute | solution.py:353
  7.0 12.7 %copy-start = (bf16[64,64,3,3]{1,0,3,2:T(8,128)(2,1)S(1)}, bf16[64,64,3,3]{1,0,3,2:T(8,128)(2,1)}, u32[]{:S(2)}) copy-start(bf16[64,64,3,3]{1,0,3,2:T(8,128)(2,1)} %param.13) | copy-start | bytes 221188
  7.0 12.7 %copy-start.1 = (bf16[64,81,3,3]{1,0,3,2:T(8,128)(2,1)S(1)}, bf16[64,81,3,3]{1,0,3,2:T(8,128)(2,1)}, u32[]{:S(2)}) copy-start(bf16[64,81,3,3]{1,0,3,2:T(8,128)(2,1)} %param.15) | copy-start | bytes 279940
  10.1 9.6 %collective-permute-start.4 = (bf16[12,32,256]{2,1,0:T(8,128)(2,1)S(1)}, bf16[12,32,256]{2,1,0:T(8,128)(2,1)S(1)}, u32[]{:S(2)}, u32[]{:S(2)}) collective-permute-start(bf16[12,32,256]{2,1,0:T(8,128)(2,1)S(1)} %constant_dynamic-update-slice_fusion.2.img_ref), channel_id=1, source_target_pairs={{1,2},{2,1},{5,6},{6,5},{9,10},{10,9},{13,14},{14,13},{17,18},{18,... | collective-permute-start | bytes 589832 | tf_op jit(solution)/shard_map/ppermute | solution.py:353
  16.3 3.3 %collective-permute-start.3 = (bf16[12,32,256]{2,1,0:T(8,128)(2,1)S(1)}, bf16[12,32,256]{2,1,0:T(8,128)(2,1)S(1)}, u32[]{:S(2)}, u32[]{:S(2)}) collective-permute-start(bf16[12,32,256]{2,1,0:T(8,128)(2,1)S(1)} %constant_dynamic-update-slice_fusion.2.img_ref), channel_id=1, source_target_pairs={{0,1},{1,0},{2,3},{3,2},{4,5},{5,4},{6,7},{7,6},{8,9},{9,8},{10,11... | collective-permute-start | bytes 589832 | tf_op jit(solution)/shard_map/ppermute | solution.py:353
  16.5 3.2 %copy-start.3 = (bf16[32,64,1,1]{1,0,3,2:T(8,128)(2,1)S(1)}, bf16[32,64,1,1]{1,0,3,2:T(8,128)(2,1)}, u32[]{:S(2)}) copy-start(bf16[32,64,1,1]{1,0,3,2:T(8,128)(2,1)} %param.14) | copy-start | bytes 12292
  16.6 3.1 %copy-start.4 = (bf16[2,64,3,3]{1,0,3,2:T(2,128)(2,1)S(1)}, bf16[2,64,3,3]{1,0,3,2:T(2,128)(2,1)}, u32[]{:S(2)}) copy-start(bf16[2,64,3,3]{1,0,3,2:T(2,128)(2,1)} %param.17) | copy-start | bytes 6916
